TPU v7x, 32 devices: a whole 2x2x4 slice. The times are simulated.
32 devices in a mesh: ctx: 8 (over z, y), shard: 4 (over x, core).
Axes of the slice: x: 2, y: 2, z: 4, core: 2. Of those that a mesh axis runs over, the one named last changes fastest.
Arguments:
- inputs: bfloat16 [4, 2048, 1152], P('shard', 'ctx'), may hold values from -6 to 6
- gain_attn: bfloat16 [1152], P('shard'), may hold values from 0.5 to 1.5
- w_query: bfloat16 [1152, 1152], P('shard'), may hold values from -0.1875 to 0.1875
- w_key: bfloat16 [1152, 384], P('shard'), may hold values from -0.1875 to 0.1875
- w_value: bfloat16 [1152, 384], P('shard'), may hold values from -0.1875 to 0.1875
- w_out: bfloat16 [1152, 1152], P('shard'), may hold values from -3 to 3
- gain_mlp: bfloat16 [1152], P('shard'), may hold values from 0.5 to 1.5
- w_gate: bfloat16 [1152, 3072], P('shard'), may hold values from -0.1875 to 0.1875
- w_up: bfloat16 [1152, 3072], P('shard'), may hold values from -0.1875 to 0.1875
- w_down: bfloat16 [3072, 1152], P('shard'), may hold values from -0.109375 to 0.109375
- cotangent: bfloat16 [4, 2048, 1152], P('shard', 'ctx'), may hold values from -6 to 6
Outputs:
- output: bfloat16 [4, 2048, 1152], P('shard', 'ctx')
- grad_inputs: bfloat16 [4, 2048, 1152], P('shard', 'ctx')
- grad_gain_attn: float32 [1152], P('shard')
- grad_w_query: float32 [1152, 1152], P('shard')
- grad_w_key: float32 [1152, 384], P('shard')
- grad_w_value: float32 [1152, 384], P('shard')
- grad_w_out: float32 [1152, 1152], P('shard')
- grad_gain_mlp: float32 [1152], P('shard')
- grad_w_gate: float32 [1152, 3072], P('shard')
- grad_w_up: float32 [1152, 3072], P('shard')
- grad_w_down: float32 [3072, 1152], P('shard')
All inputs are finite; a program needn't handle non-finite values.
Results may differ from a plain program's by a relative error of at most 0.018.
Values may be sent and summed in bfloat16 or wider, within the bound.
No kernel may reach another device: no remote copies, remote signals or barrier semaphores. Data moves between devices by JAX's collectives and lax.ppermute only.
A program may use at most 320 MiB of HBM per device.

v0:
```python
import math

import jax
import jax.numpy as jnp
from jax import lax
from jax.sharding import PartitionSpec as P

HEAD = 64
BLOCK = 256


EPSILON = 1e-05
NEGATIVE = -1e30


def normalize(values, gain):
    scale = lax.rsqrt(jnp.mean(values * values, axis=-1, keepdims=True) + EPSILON)
    return values * scale * gain


def rotate(values, positions, heads):
    count = values.shape[0]
    width = values.shape[1] // heads
    half = width // 2
    frequency = jnp.exp(jnp.arange(half, dtype=jnp.float32) * (-2.0 * math.log(10000.0) / width))
    angles = positions.astype(jnp.float32)[:, None] * frequency[None, :]
    cosine = jnp.cos(angles)[:, None, :]
    sine = jnp.sin(angles)[:, None, :]
    shaped = values.reshape(count, heads, width)
    first = shaped[..., :half]
    second = shaped[..., half:]
    turned = jnp.concatenate(
        [first * cosine - second * sine, second * cosine + first * sine], axis=-1
    )
    return turned.reshape(count, heads * width)


def scores_of(query_head_count, key_block, block_start, positions):
    count = key_block.shape[0]
    key_heads = key_block.reshape(count, query_head_count.shape[1], HEAD)
    raw = (
        jnp.einsum(
            "cngd,rnd->ngcr", query_head_count, key_heads, preferred_element_type=jnp.float32
        )
        * 0.125
    )
    key_index = block_start + jnp.arange(count, dtype=jnp.int32)
    allowed = key_index[None, :] // BLOCK <= positions[:, None] // BLOCK
    return jnp.where(allowed, raw, -jnp.inf)


def over_blocks(carry, key_rows, value_rows, key_start, step, last_block):
    total_rows = key_rows.shape[0]
    width = math.gcd(total_rows, 1024)

    def advance(index, state):
        begin = index * width
        key_block = lax.dynamic_slice_in_dim(key_rows, begin, width, 0)
        value_block = lax.dynamic_slice_in_dim(value_rows, begin, width, 0)
        block_start = key_start + begin
        return lax.cond(
            block_start // BLOCK <= last_block,
            lambda inner: step(inner, key_block, value_block, block_start),
            lambda inner: inner,
            state,
        )

    return lax.fori_loop(0, total_rows // width, advance, carry)


def on_device(
    inputs, gain_attn, w_query, w_key, w_value, w_out, gain_mlp, w_gate, w_up, w_down, cotangent
):
    count = inputs.shape[1]
    residual_in = inputs[0].astype(jnp.float32)
    gain_one, query_mat, key_mat, value_mat, output_matrix = (
        lax.all_gather(gain_attn, "shard", axis=0, tiled=True),
        lax.all_gather(w_query, "shard", axis=0, tiled=True),
        lax.all_gather(w_key, "shard", axis=0, tiled=True),
        lax.all_gather(w_value, "shard", axis=0, tiled=True),
        lax.all_gather(w_out, "shard", axis=0, tiled=True),
    )
    heads = query_mat.shape[1] // HEAD
    kv_heads = key_mat.shape[1] // HEAD
    group = heads // kv_heads
    first = lax.axis_index("ctx") * count
    positions = first + jnp.arange(count, dtype=jnp.int32)
    last_block = (first + count - 1) // BLOCK
    hidden = normalize(residual_in, gain_one.astype(jnp.float32)).astype(jnp.bfloat16)
    query_pre = jnp.dot(hidden, query_mat, preferred_element_type=jnp.float32)
    key_pre = jnp.dot(hidden, key_mat, preferred_element_type=jnp.float32)
    value_pre = jnp.dot(hidden, value_mat, preferred_element_type=jnp.float32)
    queries = rotate(query_pre, positions, heads).astype(jnp.bfloat16)
    keys = rotate(key_pre, positions, kv_heads).astype(jnp.bfloat16)
    values = value_pre.astype(jnp.bfloat16)
    query_head_count = queries.reshape(count, kv_heads, group, HEAD)

    def stat_step(state, key_block, value_block, block_start):
        top, total = state
        scores = scores_of(query_head_count, key_block, block_start, positions)
        new_top = jnp.maximum(top, jnp.max(scores, axis=-1))
        total = total * jnp.exp(top - new_top) + jnp.sum(
            jnp.exp(scores - new_top[..., None]), axis=-1
        )
        return (new_top, total)

    def make_out(log_total):

        def out_step(weighted, key_block, value_block, block_start):
            scores = scores_of(query_head_count, key_block, block_start, positions)
            weights = jnp.exp(scores - log_total[..., None]).astype(jnp.bfloat16)
            value_heads = value_block.reshape(value_block.shape[0], kv_heads, HEAD)
            return weighted + jnp.einsum(
                "ngcr,rnd->cngd", weights, value_heads, preferred_element_type=jnp.float32
            )

        return out_step

    start_stats = (
        jnp.full((kv_heads, group, count), NEGATIVE, jnp.float32),
        jnp.zeros((kv_heads, group, count), jnp.float32),
    )
    initial_output = jnp.zeros((count, kv_heads, group, HEAD), jnp.float32)
    piece = lax.all_gather(keys, "ctx", axis=0, tiled=True)
    top, total = over_blocks(start_stats, piece, piece, jnp.int32(0), stat_step, last_block)
    log_total = top + jnp.log(total)
    out_step = make_out(log_total)
    weighted = over_blocks(
        initial_output,
        lax.all_gather(keys, "ctx", axis=0, tiled=True),
        lax.all_gather(values, "ctx", axis=0, tiled=True),
        jnp.int32(0),
        out_step,
        last_block,
    )
    attended = weighted.reshape(count, heads * HEAD).astype(jnp.bfloat16)
    mid = residual_in + jnp.dot(attended, output_matrix, preferred_element_type=jnp.float32)
    gain_two, gate_mat, up_mat, down_mat = (
        lax.all_gather(gain_mlp, "shard", axis=0, tiled=True),
        lax.all_gather(w_gate, "shard", axis=0, tiled=True),
        lax.all_gather(w_up, "shard", axis=0, tiled=True),
        lax.all_gather(w_down, "shard", axis=0, tiled=True),
    )
    normed = normalize(mid, gain_two.astype(jnp.float32)).astype(jnp.bfloat16)
    gate = jnp.dot(normed, gate_mat, preferred_element_type=jnp.float32)
    up = jnp.dot(normed, up_mat, preferred_element_type=jnp.float32)
    activated = (jax.nn.silu(gate) * up).astype(jnp.bfloat16)
    result = mid + jnp.dot(activated, down_mat, preferred_element_type=jnp.float32)
    output = result.astype(jnp.bfloat16)[None]
    grad_result = cotangent[0]
    grad_w_down = jnp.einsum(
        "cf,cd->fd", activated, grad_result, preferred_element_type=jnp.float32
    )
    grad_activated = jnp.einsum(
        "cd,fd->cf", grad_result, down_mat, preferred_element_type=jnp.float32
    )
    _, pull_gate = jax.vjp(lambda gate_in, up_in: jax.nn.silu(gate_in) * up_in, gate, up)
    grad_gate, grad_up = pull_gate(grad_activated)
    grad_gate = grad_gate.astype(jnp.bfloat16)
    grad_up = grad_up.astype(jnp.bfloat16)
    grad_w_gate = jnp.einsum("cd,cf->df", normed, grad_gate, preferred_element_type=jnp.float32)
    grad_w_up = jnp.einsum("cd,cf->df", normed, grad_up, preferred_element_type=jnp.float32)
    grad_normed = jnp.einsum(
        "cf,df->cd", grad_gate, gate_mat, preferred_element_type=jnp.float32
    ) + jnp.einsum("cf,df->cd", grad_up, up_mat, preferred_element_type=jnp.float32)
    _, pull_norm = jax.vjp(normalize, mid, gain_two.astype(jnp.float32))
    grad_mid_norm, grad_gain_two = pull_norm(grad_normed)
    grad_mid = grad_result.astype(jnp.float32) + grad_mid_norm
    grad_branch = grad_mid.astype(jnp.bfloat16)
    grad_w_out = jnp.einsum("cq,cd->qd", attended, grad_branch, preferred_element_type=jnp.float32)
    grad_attended = jnp.einsum(
        "cd,qd->cq", grad_branch, output_matrix, preferred_element_type=jnp.float32
    ).astype(jnp.bfloat16)
    grad_heads = grad_attended.reshape(count, kv_heads, group, HEAD)
    all_keys, all_values = (
        lax.all_gather(keys, "ctx", axis=0, tiled=True),
        lax.all_gather(values, "ctx", axis=0, tiled=True),
    )

    def delta_step(delta, key_block, value_block, block_start):
        scores = scores_of(query_head_count, key_block, block_start, positions)
        probs = jnp.exp(scores - log_total[..., None])
        value_heads = value_block.reshape(value_block.shape[0], kv_heads, HEAD)
        grad_probs = jnp.einsum(
            "cngd,rnd->ngcr", grad_heads, value_heads, preferred_element_type=jnp.float32
        )
        return delta + jnp.sum(probs * grad_probs, axis=-1)

    delta = over_blocks(
        jnp.zeros((kv_heads, group, count), jnp.float32),
        all_keys,
        all_values,
        0,
        delta_step,
        last_block,
    )

    def grad_step(state, key_block, value_block, block_start):
        query_grad, buffer = state
        block_count = key_block.shape[0]
        scores = scores_of(query_head_count, key_block, block_start, positions)
        probs = jnp.exp(scores - log_total[..., None])
        key_heads = key_block.reshape(block_count, kv_heads, HEAD)
        value_heads = value_block.reshape(block_count, kv_heads, HEAD)
        grad_probs = jnp.einsum(
            "cngd,rnd->ngcr", grad_heads, value_heads, preferred_element_type=jnp.float32
        )
        grad_scores = (probs * (grad_probs - delta[..., None])).astype(jnp.bfloat16)
        query_grad = query_grad + jnp.einsum(
            "ngcr,rnd->cngd", grad_scores, key_heads, preferred_element_type=jnp.float32
        )
        key_gradient = jnp.einsum(
            "ngcr,cngd->rnd", grad_scores, query_head_count, preferred_element_type=jnp.float32
        )
        grad_value = jnp.einsum(
            "ngcr,cngd->rnd",
            probs.astype(jnp.bfloat16),
            grad_heads,
            preferred_element_type=jnp.float32,
        )
        piece = jnp.concatenate(
            [
                key_gradient.reshape(block_count, kv_heads * HEAD) * 0.125,
                grad_value.reshape(block_count, kv_heads * HEAD),
            ],
            axis=1,
        )
        return (query_grad, lax.dynamic_update_slice_in_dim(buffer, piece, block_start, 0))

    initial_gradient = (
        jnp.zeros((count, kv_heads, group, HEAD), jnp.float32),
        jnp.zeros((all_keys.shape[0], 2 * kv_heads * HEAD), jnp.float32),
    )
    query_grad, buffer = over_blocks(
        initial_gradient, all_keys, all_values, 0, grad_step, last_block
    )
    own_grads = lax.psum_scatter(buffer, "ctx", scatter_dimension=0, tiled=True)
    grad_queries = query_grad.reshape(count, heads * HEAD) * 0.125
    _, pull_query = jax.vjp(lambda part: rotate(part, positions, heads), query_pre)
    _, pull_key = jax.vjp(lambda part: rotate(part, positions, kv_heads), key_pre)
    grad_query_pre = pull_query(grad_queries)[0].astype(jnp.bfloat16)
    grad_key_pre = pull_key(own_grads[:, : kv_heads * HEAD])[0].astype(jnp.bfloat16)
    grad_value_pre = own_grads[:, kv_heads * HEAD :].astype(jnp.bfloat16)
    grad_w_query = jnp.einsum(
        "cd,cq->dq", hidden, grad_query_pre, preferred_element_type=jnp.float32
    )
    grad_w_key = jnp.einsum("cd,cq->dq", hidden, grad_key_pre, preferred_element_type=jnp.float32)
    grad_w_value = jnp.einsum(
        "cd,cq->dq", hidden, grad_value_pre, preferred_element_type=jnp.float32
    )
    grad_hidden = (
        jnp.einsum("cq,dq->cd", grad_query_pre, query_mat, preferred_element_type=jnp.float32)
        + jnp.einsum("cq,dq->cd", grad_key_pre, key_mat, preferred_element_type=jnp.float32)
        + jnp.einsum("cq,dq->cd", grad_value_pre, value_mat, preferred_element_type=jnp.float32)
    )
    _, pull_first = jax.vjp(normalize, residual_in, gain_one.astype(jnp.float32))
    grad_in_norm, grad_gain_one = pull_first(grad_hidden)
    grad_inputs = (grad_mid + grad_in_norm).astype(jnp.bfloat16)[None]
    parts = (
        lax.psum_scatter(
            grad_gain_one.astype(jnp.bfloat16), "shard", scatter_dimension=0, tiled=True
        ).astype(jnp.float32),
        lax.psum_scatter(
            grad_w_query.astype(jnp.bfloat16), "shard", scatter_dimension=0, tiled=True
        ).astype(jnp.float32),
        lax.psum_scatter(
            grad_w_key.astype(jnp.bfloat16), "shard", scatter_dimension=0, tiled=True
        ).astype(jnp.float32),
        lax.psum_scatter(
            grad_w_value.astype(jnp.bfloat16), "shard", scatter_dimension=0, tiled=True
        ).astype(jnp.float32),
        lax.psum_scatter(
            grad_w_out.astype(jnp.bfloat16), "shard", scatter_dimension=0, tiled=True
        ).astype(jnp.float32),
        lax.psum_scatter(
            grad_gain_two.astype(jnp.bfloat16), "shard", scatter_dimension=0, tiled=True
        ).astype(jnp.float32),
        lax.psum_scatter(
            grad_w_gate.astype(jnp.bfloat16), "shard", scatter_dimension=0, tiled=True
        ).astype(jnp.float32),
        lax.psum_scatter(
            grad_w_up.astype(jnp.bfloat16), "shard", scatter_dimension=0, tiled=True
        ).astype(jnp.float32),
        lax.psum_scatter(
            grad_w_down.astype(jnp.bfloat16), "shard", scatter_dimension=0, tiled=True
        ).astype(jnp.float32),
    )
    summed = lax.psum(
        (parts[0], parts[1], parts[2], parts[3], parts[4], parts[5], parts[6], parts[7], parts[8]),
        "ctx",
    )
    return (
        output,
        grad_inputs,
        summed[0],
        summed[1],
        summed[2],
        summed[3],
        summed[4],
        summed[5],
        summed[6],
        summed[7],
        summed[8],
    )


def solution(mesh):
    placed = (
        P("shard", "ctx", None),
        P("shard"),
        P("shard", None),
        P("shard", None),
        P("shard", None),
        P("shard", None),
        P("shard"),
        P("shard", None),
        P("shard", None),
        P("shard", None),
        P("shard", "ctx", None),
    )
    return jax.shard_map(
        on_device,
        mesh=mesh,
        in_specs=placed,
        out_specs=(
            P("shard", "ctx", None),
            P("shard", "ctx", None),
            P("shard"),
            P("shard", None),
            P("shard", None),
            P("shard", None),
            P("shard", None),
            P("shard"),
            P("shard", None),
            P("shard", None),
            P("shard", None),
        ),
        check_vma=False,
    )
```

profile of v0, /device:TPU:9, one launch (start us, length us, event | category | flops | bytes accessed | tf_op | source)
XLA Modules:
  0.0 1466.1 jit_solution(11560700565964744816)
XLA Ops:
  7.2 1.3 fusion.92
  11.0 5.8 all-reduce.10
  18.1 10.1 all_gather.40
  31.2 9.3 all_gather.37
  45.5 29.7 %all-gather.12.cloned.1.call-done = bf16[2048,384]{1,0:T(8,128)(2,1)} async-done(((bf16[256,384]{1,0:T(8,128)(2,1)}), bf16[2048,384]{1,0:T(8,128)(2,1)}) %all-gather.12.cloned.1.call-update) | async-done | bytes 1572880 | tf_op jit(solution)/shard_map/all_gather | solution.py:131
  75.2 1.7 copy.50
  76.9 25.1 %all-gather.10.cloned.1.call-done = bf16[1152,1152]{1,0:T(8,128)(2,1)} async-done(((bf16[288,1152]{1,0:T(8,128)(2,1)}), bf16[1152,1152]{1,0:T(8,128)(2,1)}) %all-gather.10.cloned.1.call-update) | async-done | bytes 2654224 | tf_op jit(solution)/shard_map/all_gather | solution.py:78
  102.0 5.2 copy.49
  107.2 2.8 fusion.76
  110.3 36.7 %all-gather.8.cloned.1.call-done = bf16[2048,384]{0,1:T(8,128)(2,1)} async-done(((bf16[256,384]{0,1:T(8,128)(2,1)}), bf16[2048,384]{0,1:T(8,128)(2,1)}) %all-gather.8.cloned.1.call-update) | async-done | bytes 1572880 | tf_op jit(solution)/shard_map/all_gather | solution.py:130
  147.1 20.5 %while.74 = (s32[]{:T(128)}, f32[6,3,256]{2,1,0:T(4,128)S(1)}, f32[6,3,256]{2,1,0:T(4,128)S(1)}, s32[]{:T(128)}, bf16[2048,384]{0,1:T(8,128)(2,1)}, /*index=5*/b...) while((s32[]{:T(128)}, f32[6,3,256]{2,1,0:T(4,128)S(1)}, ...), condition=%wide.region_6.7_spmd.clone, body=%wide.region_1.6_spmd.clone.sunk | while | flops 637301760 | bytes 41736640 | solution.py:68
  147.1 20.3 %conditional.12 = ((f32[6,3,256]{2,1,0:T(4,128)S(1)}, f32[6,3,256]{2,1,0:T(4,128)S(1)})) conditional(s32[]{:T(128)} %convert_element_type.371, (f32[6,3,256]{2,1,0:T(4,128)S(1)}, f32[6,3,256]{2,1,0:T(4,128)S(1)}) %tuple.257, (s32[]{:T(128)}, s32[]{:T(128)}, pred[]{:T(512)}, bf16[2048,384]{0,1:T(8,128)(2,1)}, bf16[256,6,3,64]{0,3,2,1:T(8,128)(2,1)S(1)}, ...), branch_computations={%region_2.2_spmd, %region_3.5_spmd} | conditional | flops 637301760 | bytes 41735228 | solution.py:61
  148.6 8.2 fusion.8
  156.8 10.6 exponential_reduce_fusion
  169.3 11.7 while.75
  169.5 11.4 conditional.13
  169.6 2.2 constant_dynamic-slice_fusion.1
  172.7 8.3 fusion.23
  181.0 1.9 convert_element_type.224
  182.9 3.4 multiply_reduce_fusion.2
  187.6 40.1 %all-gather.16.cloned.1.call-done = bf16[1152,3072]{1,0:T(8,128)(2,1)} async-done(((bf16[288,3072]{1,0:T(8,128)(2,1)}), bf16[1152,3072]{1,0:T(8,128)(2,1)}) %all-gather.16.cloned.1.call-update) | async-done | bytes 7077904 | tf_op jit(solution)/shard_map/all_gather | solution.py:140
  227.7 6.9 fusion.95
  234.5 45.4 %all-gather.18.cloned.1.call-done = bf16[1152,3072]{1,0:T(8,128)(2,1)} async-done(((bf16[288,3072]{1,0:T(8,128)(2,1)}), bf16[1152,3072]{1,0:T(8,128)(2,1)}) %all-gather.18.cloned.1.call-update) | async-done | bytes 7077904 | tf_op jit(solution)/shard_map/all_gather | solution.py:141
  280.0 6.9 fusion.96
  286.8 45.6 %all-gather.20.cloned.1.call-done = bf16[3072,1152]{1,0:T(8,128)(2,1)} async-done(((bf16[768,1152]{1,0:T(8,128)(2,1)}), bf16[3072,1152]{1,0:T(8,128)(2,1)}) %all-gather.20.cloned.1.call-update) | async-done | bytes 7077904 | tf_op jit(solution)/shard_map/all_gather | solution.py:142
  332.4 10.3 multiply_convert_fusion
  342.7 6.4 fusion.97
  349.2 3.1 multiply_reduce_fusion
  356.0 10.3 while.76
  356.0 10.2 conditional.14
  357.2 2.7 fusion.93
  360.2 6.0 fusion.31
  367.2 3.4 broadcast_in_dim.106
  370.6 43.9 %while.77 = (s32[]{:T(128)}, f32[256,6,3,64]{0,3,2,1:T(8,128)S(1)}, f32[2048,768]{0,1:T(8,128)}, s32[]{:T(128)}, bf16[2048,384]{0,1:T(8,128)(2,1)S(1)}, /*index=...) while((s32[]{:T(128)}, f32[256,6,3,64]{0,3,2,1:T(8,128)S(1)}, ...), condition=%wide.region_21.22_spmd.clone, body=%wide.region_18.21_spmd.clone.sunk | while | flops 3068841984 | bytes 152898224 | solution.py:68
  370.8 43.7 %conditional.15 = ((f32[256,6,3,64]{0,3,2,1:T(8,128)S(1)}, f32[2048,768]{0,1:T(8,128)})) conditional(s32[]{:T(128)} %convert_element_type.374, (f32[256,6,3,64]{0,3,2,1:T(8,128)S(1)}, f32[2048,768]{0,1:T(8,128)}) %tuple.264, (s32[]{:T(128)}, s32[]{:T(128)}, pred[]{:T(512)}, bf16[2048,384]{0,1:T(8,128)(2,1)S(1)}, ...), branch_computations={%region_19.19_spmd, %region_20.20_spmd} | conditional | flops 3068841984 | bytes 152896736 | solution.py:61
  372.1 7.9 fusion.94
  380.3 9.4 fusion.38
  389.8 1.8 fusion.45
  391.6 1.8 copy-done
  393.4 12.2 fusion.42
  405.6 6.7 bitcast_multiply_fusion.1
  412.4 2.2 maximum_dynamic-update-slice_fusion
  416.5 2.6 convolution_convert_fusion.4
  420.5 2.4 convolution_convert_fusion.3
  424.0 6.3 convolution_convert_fusion.2
  430.3 6.4 convolution_convert_fusion.1
  436.8 1.3 copy-done.19
  438.1 6.2 convolution_convert_fusion
  444.3 141.2 %reduce-scatter.9.cloned.1.call-done = f32[256,768]{0,1:T(8,128)} async-done(((f32[2048,768]{0,1:T(8,128)}), f32[256,768]{0,1:T(8,128)}) %reduce-scatter.9.cloned.1.call-update) | async-done | bytes 786448 | tf_op jit(solution)/shard_map/reduce_scatter | solution.py:237
  586.7 1.5 convolution_convert_fusion.6
  589.1 6.6 fusion.56
  595.7 1.5 convolution_convert_fusion.5
  597.3 4.1 fusion.98
  601.4 22.3 %reduce-scatter.11.cloned.1.call-done = bf16[288,1152]{1,0:T(8,128)(2,1)} async-done(((bf16[1152,1152]{1,0:T(8,128)(2,1)}), bf16[288,1152]{1,0:T(8,128)(2,1)}) %reduce-scatter.11.cloned.1.call-update) | async-done | bytes 663568 | tf_op jit(solution)/shard_map/reduce_scatter | solution.py:263
  623.7 38.1 %reduce-scatter.17.cloned.1.call-done = bf16[288,1152]{1,0:T(8,128)(2,1)} async-done(((bf16[1152,1152]{1,0:T(8,128)(2,1)}), bf16[288,1152]{1,0:T(8,128)(2,1)}) %reduce-scatter.17.cloned.1.call-update) | async-done | bytes 663568 | tf_op jit(solution)/shard_map/reduce_scatter | solution.py:272
  661.8 1.8 convolution_add_fusion.1
  663.6 2.0 fusion.64
  665.6 5.9 all-reduce.9
  672.8 55.2 %reduce-scatter.19.cloned.1.call-done = bf16[288,3072]{1,0:T(8,128)(2,1)} async-done(((bf16[1152,3072]{1,0:T(8,128)(2,1)}), bf16[288,3072]{1,0:T(8,128)(2,1)}) %reduce-scatter.19.cloned.1.call-update) | async-done | bytes 1769488 | tf_op jit(solution)/shard_map/reduce_scatter | solution.py:278
  728.0 66.2 %reduce-scatter.21.cloned.1.call-done = bf16[288,3072]{1,0:T(8,128)(2,1)} async-done(((bf16[1152,3072]{1,0:T(8,128)(2,1)}), bf16[288,3072]{1,0:T(8,128)(2,1)}) %reduce-scatter.21.cloned.1.call-update) | async-done | bytes 1769488 | tf_op jit(solution)/shard_map/reduce_scatter | solution.py:281
  794.2 66.2 %reduce-scatter.23.cloned.1.call-done = bf16[768,1152]{1,0:T(8,128)(2,1)} async-done(((bf16[3072,1152]{1,0:T(8,128)(2,1)}), bf16[768,1152]{1,0:T(8,128)(2,1)}) %reduce-scatter.23.cloned.1.call-update) | async-done | bytes 1769488 | tf_op jit(solution)/shard_map/reduce_scatter | solution.py:284
  860.4 27.1 %reduce-scatter.13.cloned.1.call-done = bf16[288,384]{1,0:T(8,128)(2,1)} async-done(((bf16[1152,384]{1,0:T(8,128)(2,1)}), bf16[288,384]{1,0:T(8,128)(2,1)}) %reduce-scatter.13.cloned.1.call-update) | async-done | bytes 221200 | tf_op jit(solution)/shard_map/reduce_scatter | solution.py:266
  887.4 26.9 %reduce-scatter.15.cloned.1.call-done = bf16[288,384]{1,0:T(8,128)(2,1)} async-done(((bf16[1152,384]{1,0:T(8,128)(2,1)}), bf16[288,384]{1,0:T(8,128)(2,1)}) %reduce-scatter.15.cloned.1.call-update) | async-done | bytes 221200 | tf_op jit(solution)/shard_map/reduce_scatter | solution.py:269
  914.3 544.8 %all-reduce.12 = (f32[288]{0:T(512)}, f32[288,1152]{1,0:T(8,128)}, f32[288,384]{1,0:T(8,128)}, f32[288,384]{1,0:T(8,128)}, f32[288,1152]{1,0:T(8,128)}, /*index=...) all-reduce(f32[288]{0:T(512)S(1)} %get-tuple-element.1598, ...), channel_id=1, replica_groups=mesh['ctx'=8,'shard'=4] {'ctx'}, use_global_device_ids=true, to_apply=%region_26.27 | all-reduce | flops 3539520 | bytes 21238272 | tf_op jit(solution)/shard_map/psum | solution.py:288
  (185 shorter events, 31.4 us)
Async XLA Ops:
  7.2 21.9 %copy-start.6 = (bf16[1,256,1152]{2,1,0:T(8,128)(2,1)S(1)}, bf16[1,256,1152]{2,1,0:T(8,128)(2,1)}, u32[]{:S(2)}) copy-start(bf16[1,256,1152]{2,1,0:T(8,128)(2,1)} %param.27) | copy-start | bytes 1769476
  7.2 68.0 %all-gather.12.cloned.1.call-start = ((), (), s32[]{:S(2)}) async-start(), calls=%async_computation.10 | async-start | bytes 1769472 | tf_op jit(solution)/shard_map/all_gather | solution.py:131
  16.8 90.5 %copy-start.33 = (f32[1152]{0:T(1024)}, f32[1152]{0:T(1024)S(1)}, u32[]{:S(2)}) copy-start(f32[1152]{0:T(1024)S(1)} %convert_element_type.216) | copy-start | bytes 13828
  18.0 12.3 copy-start.38
  18.1 89.2 %copy-start.35 = (f32[256]{0:T(256)}, f32[256]{0:T(256)S(1)}, u32[]{:S(2)}) copy-start(f32[256]{0:T(256)S(1)} %fusion.86) | copy-start | bytes 3076
  28.2 0.9 copy-start.18
  29.1 2.1 copy-start.32
  30.4 71.6 %all-gather.10.cloned.1.call-start = ((), (), s32[]{:S(2)}) async-start(), calls=%async_computation.9 | async-start | bytes 3317760 | tf_op jit(solution)/shard_map/all_gather | solution.py:78
  31.1 115.9 %all-gather.8.cloned.1.call-start = ((), (), s32[]{:S(2)}) async-start(), calls=%async_computation.8 | async-start | bytes 1769472 | tf_op jit(solution)/shard_map/all_gather | solution.py:130
  40.5 1.7 copy-start.10
  41.6 68.5 %copy-start.28 = (f32[256,32]{0,1:T(8,128)}, f32[256,32]{0,1:T(8,128)S(1)}, u32[]{:S(2)}) copy-start(f32[256,32]{0,1:T(8,128)S(1)} %get-tuple-element.1589) | copy-start | bytes 98308
  41.6 68.5 %copy-start.30 = (f32[256,32]{0,1:T(8,128)}, f32[256,32]{0,1:T(8,128)S(1)}, u32[]{:S(2)}) copy-start(f32[256,32]{0,1:T(8,128)S(1)} %get-tuple-element.1590) | copy-start | bytes 98308
  42.9 140.0 %all-gather.14.cloned.1.call-start = ((), (), s32[]{:S(2)}) async-start(), calls=%async_computation.11 | async-start | bytes 3317760 | tf_op jit(solution)/shard_map/all_gather | solution.py:81
  43.5 184.2 %all-gather.16.cloned.1.call-start = ((), (), s32[]{:S(2)}) async-start(), calls=%async_computation.12 | async-start | bytes 8847360 | tf_op jit(solution)/shard_map/all_gather | solution.py:140
  44.1 235.9 %all-gather.18.cloned.1.call-start = ((), (), s32[]{:S(2)}) async-start(), calls=%async_computation.13 | async-start | bytes 8847360 | tf_op jit(solution)/shard_map/all_gather | solution.py:141
  44.6 287.7 %all-gather.20.cloned.1.call-start = ((), (), s32[]{:S(2)}) async-start(), calls=%async_computation.14 | async-start | bytes 8847360 | tf_op jit(solution)/shard_map/all_gather | solution.py:142
  45.4 540.2 %reduce-scatter.9.cloned.1.call-start = ((), (), s32[]{:S(2)}) async-start(), calls=%async_computation.15 | async-start | bytes 7077888 | tf_op jit(solution)/shard_map/reduce_scatter | solution.py:237
  181.0 5.4 copy-start.2
  182.9 3.4 copy-start.21
  186.4 1.0 copy-start.15
  187.5 92.4 %copy-start.12 = (bf16[256,1152]{1,0:T(8,128)(2,1)}, bf16[256,1152]{1,0:T(8,128)(2,1)S(1)}, u32[]{:S(2)}) copy-start(bf16[256,1152]{1,0:T(8,128)(2,1)S(1)} %multiply_convert_fusion.2) | copy-start | bytes 1769476
  234.5 97.9 %copy-start.20 = (bf16[1,256,1152]{2,1,0:T(8,128)(2,1)S(1)}, bf16[1,256,1152]{2,1,0:T(8,128)(2,1)}, u32[]{:S(2)}) copy-start(bf16[1,256,1152]{2,1,0:T(8,128)(2,1)} %param.37) | copy-start | bytes 1769476
  342.7 6.4 copy-start.27
  342.7 6.4 copy-start.26
  342.7 6.4 copy-start.16
  342.7 6.5 copy-start.41
  352.4 2.2 copy-start.42
  352.7 1.0 copy-start.8
  354.5 1.4 copy-start.1
  354.5 1.4 copy-start.37
  366.3 0.8 copy-start.4
  372.1 8.2 copy-start.5
  380.3 9.5 copy-start.14
  389.8 3.6 copy-start
  405.6 6.7 copy-start.3
  414.6 0.8 copy-start.29
  414.6 0.8 copy-start.31
  414.6 209.1 %reduce-scatter.11.cloned.1.call-start = ((), (), s32[]{:S(2)}) async-start(), calls=%async_computation.16 | async-start | bytes 3317760 | tf_op jit(solution)/shard_map/reduce_scatter | solution.py:263
  415.3 1.1 copy-start.7
  415.3 1.1 copy-start.34
  415.4 1.1 copy-start.36
  415.6 0.8 copy-start.23
  419.1 1.3 copy-start.9
  419.1 1.4 copy-start.22
  419.1 242.7 %reduce-scatter.17.cloned.1.call-start = ((), (), s32[]{:S(2)}) async-start(), calls=%async_computation.19 | async-start | bytes 3317760 | tf_op jit(solution)/shard_map/reduce_scatter | solution.py:272
  422.9 1.1 copy-start.13
  422.9 305.0 %reduce-scatter.19.cloned.1.call-start = ((), (), s32[]{:S(2)}) async-start(), calls=%async_computation.20 | async-start | bytes 8847360 | tf_op jit(solution)/shard_map/reduce_scatter | solution.py:278
  430.3 363.9 %reduce-scatter.21.cloned.1.call-start = ((), (), s32[]{:S(2)}) async-start(), calls=%async_computation.21 | async-start | bytes 8847360 | tf_op jit(solution)/shard_map/reduce_scatter | solution.py:281
  436.7 1.4 copy-start.19
  436.7 423.6 %reduce-scatter.23.cloned.1.call-start = ((), (), s32[]{:S(2)}) async-start(), calls=%async_computation.22 | async-start | bytes 8847360 | tf_op jit(solution)/shard_map/reduce_scatter | solution.py:284
  444.3 443.1 %reduce-scatter.13.cloned.1.call-start = ((), (), s32[]{:S(2)}) async-start(), calls=%async_computation.17 | async-start | bytes 1105920 | tf_op jit(solution)/shard_map/reduce_scatter | solution.py:266
  586.7 2.4 copy-start.17
  588.3 326.0 %reduce-scatter.15.cloned.1.call-start = ((), (), s32[]{:S(2)}) async-start(), calls=%async_computation.18 | async-start | bytes 1105920 | tf_op jit(solution)/shard_map/reduce_scatter | solution.py:269
  589.1 6.6 copy-start.25
  595.7 1.5 copy-start.24
  597.3 64.5 %copy-start.11 = (bf16[1152,384]{1,0:T(8,128)(2,1)S(1)}, bf16[1152,384]{1,0:T(8,128)(2,1)}, u32[]{:S(2)}) copy-start(bf16[1152,384]{1,0:T(8,128)(2,1)} %copy-done.10) | copy-start | bytes 2654212
  663.6 2.1 copy-start.40
  663.6 8.0 copy-start.39
Sparse Core Ops, SparseCore 0:
  30.5 44.6 all-gather.11
  76.7 25.2 all-gather.9
  104.6 42.3 all-gather.7
  148.5 26.8 all-gather.13
  176.7 50.8 all-gather.15
  229.1 50.8 all-gather.17
  281.5 50.8 all-gather.19
  414.7 170.8 reduce-scatter.8
  588.7 34.9 reduce-scatter.10
  626.8 34.8 reduce-scatter.16
  664.3 63.6 reduce-scatter.18
  730.5 63.6 reduce-scatter.20
  796.7 63.5 reduce-scatter.22
  863.5 23.8 reduce-scatter.12
  890.4 23.8 reduce-scatter.14
where the time goes:
time: 1480 us; the launch traced here: 1470 us
  waiting for transfers between devices  669 us (45%)
  blocking collectives  576 us (39%)
  matrix products  147 us (10%)
  local copies, waits for them, and re-layouts  34.2 us (2%)
  other arithmetic  21.7 us (1%)
  between operations  16.2 us (1%)
    psum x1, blocking collectives, on_device(): lax.psum((parts[0], parts[1], parts[2], parts[3], parts[4], parts[5], par...  545 us
    reduce_scatter x1, waiting for transfers between devices, on_device(): own_grads = lax.psum_scatter(buffer, 'ctx', scatter_dimension=0, tiled=True)  141 us
    reduce_scatter x1, waiting for transfers between devices, on_device(): lax.psum_scatter(grad_w_up.astype(jnp.bfloat16), 'shard', scatter_dimensi...  66.2 us
    reduce_scatter x1, waiting for transfers between devices, on_device(): lax.psum_scatter(grad_w_down.astype(jnp.bfloat16), 'shard', scatter_dimen...  66.2 us
    reduce_scatter x1, waiting for transfers between devices, on_device(): lax.psum_scatter(grad_w_gate.astype(jnp.bfloat16), 'shard', scatter_dimen...  55.2 us
    all_gather x1, waiting for transfers between devices, on_device(): lax.all_gather(w_down, 'shard', axis=0, tiled=True)  45.6 us
    all_gather x1, waiting for transfers between devices, on_device(): lax.all_gather(w_up, 'shard', axis=0, tiled=True)  45.4 us
    all_gather x1, waiting for transfers between devices, on_device(): lax.all_gather(w_gate, 'shard', axis=0, tiled=True)  40.1 us
  transfers between devices with their start and end apart: 15, of which 14 were waited for; matrix products, arithmetic and copies ran while one was open for 7% of the time, Pallas kernels for 0%

commit v1 on v0

v1 whole, which is shorter than its diff:
```python
import functools
import math

import jax
import jax.numpy as jnp
from jax import lax
from jax.experimental import pallas as pl
from jax.experimental.pallas import tpu as pltpu
from jax.sharding import PartitionSpec as P

HEAD = 64
BLOCK = 256
EPSILON = 1e-05
LANES = 128
F32 = jnp.float32
BF16 = jnp.bfloat16
SCORE_SCALE = math.log2(math.e) * 0.125
NEGATIVE = -1e30
VMEM_BYTES = 44 * 1024 * 1024


def nn(left, right):
    return lax.dot_general(left, right, (((1,), (0,)), ((), ())), preferred_element_type=F32)


def nt(left, right):
    return lax.dot_general(left, right, (((1,), (1,)), ((), ())), preferred_element_type=F32)


def tn(left, right):
    return lax.dot_general(left, right, (((0,), (0,)), ((), ())), preferred_element_type=F32)


def ring_order(count):
    if count % 2:
        return list(range(count))
    return list(range(0, count, 2)) + list(range(count - 1, 0, -2))


def params(**kwargs):
    return pltpu.CompilerParams(vmem_limit_bytes=VMEM_BYTES, **kwargs)


def cost(flops, moved, exps=0):
    return pl.CostEstimate(flops=int(flops), bytes_accessed=int(moved), transcendentals=int(exps))


VMEM_SPEC = pl.BlockSpec(memory_space=pltpu.VMEM)
SMEM_SPEC = pl.BlockSpec(memory_space=pltpu.SMEM)


def swap_halves(tile):
    lane = lax.broadcasted_iota(jnp.int32, tile.shape, 1)
    ahead = pltpu.roll(tile, LANES - HEAD // 2, 1)
    behind = pltpu.roll(tile, HEAD // 2, 1)
    return jnp.where(lane % HEAD < HEAD // 2, ahead, behind)


def assemble(shard, pieces, whole, rows):
    for hop, piece in enumerate(pieces):
        start = pl.multiple_of((shard ^ hop) * rows, 16)
        whole[pl.ds(start, rows), :] = piece[:rows, :]


def keys_kernel(shard_ref, x_ref, gain_ref, cos_ref, sin_ref, *rest, rows, kvw):
    pieces, (hidden_ref, kv_ref, whole) = rest[:-3], rest[-3:]
    x = x_ref[...].astype(F32)
    scale = lax.rsqrt(jnp.mean(x * x, axis=-1, keepdims=True) + EPSILON)
    hidden = (x * scale * gain_ref[...]).astype(BF16)
    hidden_ref[...] = hidden
    assemble(shard_ref[0], pieces, whole, rows)
    pre = nn(hidden, whole[...])
    for start in range(0, kvw, LANES):
        tile = pre[:, start : start + LANES]
        turned = tile * cos_ref[...] + swap_halves(tile) * sin_ref[...]
        kv_ref[:, start : start + LANES] = turned.astype(BF16)
    kv_ref[:, kvw:] = pre[:, kvw:].astype(BF16)


def queries_kernel(shard_ref, hidden_ref, cos_ref, sin_ref, *rest, rows):
    pieces, (query_ref, whole) = rest[:-2], rest[-2:]
    assemble(shard_ref[0], pieces, whole, rows)
    pre = nn(hidden_ref[...], whole[...])
    for start in range(0, pre.shape[1], LANES):
        tile = pre[:, start : start + LANES]
        turned = tile * cos_ref[...] + swap_halves(tile) * sin_ref[...]
        query_ref[:, start : start + LANES] = turned.astype(BF16)


def attend_kernel(
    table_ref,
    q_ref,
    kv_ref,
    x_ref,
    gain_ref,
    *rest,
    rows,
    groups,
    per,
    blocks,
):
    pieces = rest[:-10]
    (
        out_ref,
        attended_ref,
        log_ref,
        mid_ref,
        normed_ref,
        turned_q,
        acc,
        top,
        total,
        whole,
    ) = rest[-10:]
    step = pl.program_id(0)
    last = table_ref[blocks]
    shard = table_ref[blocks + 1]
    count = q_ref.shape[0]
    kvw = groups * HEAD

    @pl.when(step == 0)
    def _():
        for group in range(groups):
            for member in range(per):
                head = group * per + member
                part = q_ref[:, head * HEAD : (head + 1) * HEAD]
                turned_q[group, :, member * count : (member + 1) * count] = part.T
        acc[...] = jnp.zeros_like(acc)
        total[...] = jnp.zeros_like(total)
        top[...] = jnp.full_like(top, NEGATIVE)

    @pl.when(step <= last)
    def _():
        for group in range(groups):
            key = kv_ref[:, group * HEAD : (group + 1) * HEAD]
            value = kv_ref[:, kvw + group * HEAD : kvw + (group + 1) * HEAD]
            scores = nn(key, turned_q[group]) * SCORE_SCALE
            old = top[group : group + 1, :]
            new = jnp.maximum(old, jnp.max(scores, axis=0, keepdims=True))
            shrink = jnp.exp2(old - new)
            probs = jnp.exp2(scores - new)
            top[group : group + 1, :] = new
            total[group : group + 1, :] = total[group : group + 1, :] * shrink + jnp.sum(
                probs, axis=0, keepdims=True
            )
            acc[group] = acc[group] * shrink + tn(value, probs.astype(BF16))

    @pl.when(step == blocks - 1)
    def _():
        for group in range(groups):
            sums = total[group : group + 1, :]
            log_ref[group : group + 1, :] = top[group : group + 1, :] + jnp.log2(sums)
            rowed = acc[group] / sums
            for member in range(per):
                head = group * per + member
                out_ref[:, head * HEAD : (head + 1) * HEAD] = rowed[
                    :, member * count : (member + 1) * count
                ].T
        attended = out_ref[...].astype(BF16)
        attended_ref[...] = attended
        assemble(shard, pieces, whole, rows)
        mid = x_ref[...].astype(F32) + nn(attended, whole[...])
        mid_ref[...] = mid
        scale = lax.rsqrt(jnp.mean(mid * mid, axis=-1, keepdims=True) + EPSILON)
        normed_ref[...] = (mid * scale * gain_ref[...]).astype(BF16)


def attend_back_kernel(
    table_ref,
    q_ref,
    kv_ref,
    out_ref,
    log_ref,
    mid_ref,
    gain_ref,
    cot_ref,
    gn_ref,
    cos_ref,
    sin_ref,
    *rest,
    rows,
    groups,
    per,
    blocks,
):
    pieces = rest[:-13]
    (
        gq_ref,
        gkv_ref,
        branch_ref,
        gmid_ref,
        ggain_ref,
        whole,
        q_rows,
        q_cols,
        d_rows,
        d_cols,
        delta,
        acc,
        flat,
    ) = rest[-13:]
    step = pl.program_id(0)
    last = table_ref[blocks]
    shard = table_ref[blocks + 1]
    count = q_ref.shape[0]
    kvw = groups * HEAD

    @pl.when(step == 0)
    def _():
        mid = mid_ref[...]
        incoming = gn_ref[...]
        gain = gain_ref[...]
        scale = lax.rsqrt(jnp.mean(mid * mid, axis=-1, keepdims=True) + EPSILON)
        weighted = incoming * gain
        inner = jnp.mean(weighted * mid, axis=-1, keepdims=True)
        ggain_ref[...] = jnp.sum(incoming * mid * scale, axis=0, keepdims=True)
        grad_mid = (
            cot_ref[...].astype(F32) + scale * weighted - mid * (scale * scale * scale * inner)
        )
        gmid_ref[...] = grad_mid
        branch = grad_mid.astype(BF16)
        branch_ref[...] = branch
        assemble(shard, pieces, whole, rows)
        flat[...] = nt(branch, whole[...])
        for group in range(groups):
            for member in range(per):
                head = group * per + member
                span = slice(head * HEAD, (head + 1) * HEAD)
                cols = slice(member * count, (member + 1) * count)
                part = q_ref[:, span]
                q_rows[group, cols, :] = part
                q_cols[group, :, cols] = part.T
                grad = flat[:, span].astype(BF16)
                d_rows[group, cols, :] = grad
                d_cols[group, :, cols] = grad.T
                product = grad.astype(F32) * out_ref[:, span]
                delta[group : group + 1, cols] = jnp.sum(product.T, axis=0, keepdims=True)
        acc[...] = jnp.zeros_like(acc)

    @pl.when(step > last)
    def _():
        gkv_ref[...] = jnp.zeros_like(gkv_ref)

    @pl.when(step <= last)
    def _():
        for group in range(groups):
            key_span = slice(group * HEAD, (group + 1) * HEAD)
            value_span = slice(kvw + group * HEAD, kvw + (group + 1) * HEAD)
            key = kv_ref[:, key_span]
            value = kv_ref[:, value_span]
            scores = nn(key, q_cols[group]) * SCORE_SCALE
            probs = jnp.exp2(scores - log_ref[group : group + 1, :])
            grad_probs = nn(value, d_cols[group])
            grad_scores = (probs * (grad_probs - delta[group : group + 1, :])).astype(BF16)
            gkv_ref[:, value_span] = nn(probs.astype(BF16), d_rows[group]).astype(BF16)
            gkv_ref[:, key_span] = (nn(grad_scores, q_rows[group]) * 0.125).astype(BF16)
            acc[group] = acc[group] + tn(key, grad_scores)

    @pl.when(step == blocks - 1)
    def _():
        for group in range(groups):
            for member in range(per):
                head = group * per + member
                flat[:, head * HEAD : (head + 1) * HEAD] = (
                    acc[group, :, member * count : (member + 1) * count].T * 0.125
                )
        for start in range(0, flat.shape[1], LANES):
            tile = flat[:, start : start + LANES]
            turned = tile * cos_ref[...] - swap_halves(tile) * sin_ref[...]
            gq_ref[:, start : start + LANES] = turned.astype(BF16)


def unturn_kernel(grad_ref, cos_ref, sin_ref, out_ref, *, kvw):
    for start in range(0, kvw, LANES):
        tile = grad_ref[:, start : start + LANES].astype(F32)
        turned = tile * cos_ref[...] - swap_halves(tile) * sin_ref[...]
        out_ref[:, start : start + LANES] = turned.astype(BF16)
    out_ref[:, kvw:] = grad_ref[:, kvw:]


def inputs_kernel(shard_ref, gq_ref, gkv_ref, x_ref, gain_ref, gmid_ref, *rest, rows, hops):
    q_pieces = rest[:hops]
    kv_pieces = rest[hops : 2 * hops]
    grad_ref, ggain_ref, whole_q, whole_kv = rest[2 * hops :]
    assemble(shard_ref[0], q_pieces, whole_q, rows)
    assemble(shard_ref[0], kv_pieces, whole_kv, rows)
    incoming = nt(gq_ref[...], whole_q[...]) + nt(gkv_ref[...], whole_kv[...])
    x = x_ref[...].astype(F32)
    scale = lax.rsqrt(jnp.mean(x * x, axis=-1, keepdims=True) + EPSILON)
    weighted = incoming * gain_ref[...]
    inner = jnp.mean(weighted * x, axis=-1, keepdims=True)
    ggain_ref[...] = jnp.sum(incoming * x * scale, axis=0, keepdims=True)
    grad = gmid_ref[...] + scale * weighted - x * (scale * scale * scale * inner)
    grad_ref[...] = grad.astype(BF16)


def weight_grad_kernel(shard_ref, left_ref, right_ref, *rest, rows):
    outs, full = rest[:-1], rest[-1]
    full[...] = tn(left_ref[...], right_ref[...])
    for hop, out in enumerate(outs):
        start = pl.multiple_of((shard_ref[0] ^ hop) * rows, 8)
        out[...] = full[pl.ds(start, rows), :].astype(BF16)


def on_device(
    inputs,
    gain_attn,
    w_query,
    w_key,
    w_value,
    w_out,
    gain_mlp,
    w_gate,
    w_up,
    w_down,
    cotangent,
    *,
    n_ctx,
    n_shard,
):
    x = inputs[0]
    cot = cotangent[0]
    count, width = x.shape
    rows = w_query.shape[0]
    qw = w_query.shape[1]
    kvw = w_key.shape[1]
    ff = w_gate.shape[1]
    ff_own = w_down.shape[0]
    groups = kvw // HEAD
    per = qw // kvw
    assert count == BLOCK and n_shard == 4 and ff_own * n_shard == ff
    order = ring_order(n_ctx)
    places = [order.index(index) for index in range(n_ctx)]
    shard = lax.axis_index("shard")
    ctx = lax.axis_index("ctx")
    shard_arr = shard.astype(jnp.int32)[None]
    place = jnp.array(places, jnp.int32)[ctx]
    table = jnp.concatenate(
        [jnp.array(places, jnp.int32), jnp.stack([ctx, shard]).astype(jnp.int32)]
    )

    def hop(value, distance):
        pairs = [(index, index ^ distance) for index in range(n_shard)]
        return lax.ppermute(value, "shard", pairs)

    def gather(value):
        far = hop(value, 2)
        near = hop(value, 1)
        return [value, near, far, hop(far, 1)]

    def reduce(blocks):
        third = hop(blocks[3], 1)
        first = hop(blocks[1], 1)
        across = (blocks[2].astype(F32) + third.astype(F32)).astype(BF16)
        far = hop(across, 2)
        return blocks[0].astype(F32) + first.astype(F32) + far.astype(F32)

    def after(value, done):
        return lax.optimization_barrier((value, done))[0]

    def scatter(value):
        return lax.psum_scatter(
            value, "ctx", scatter_dimension=0, axis_index_groups=[order], tiled=False
        )

    def collect(value):
        return lax.all_gather(value, "ctx", axis=0, axis_index_groups=[order], tiled=True)

    lane = jnp.arange(LANES, dtype=jnp.int32)
    frequency = jnp.exp(
        (lane % (HEAD // 2)).astype(F32) * (-2.0 * math.log(10000.0) / HEAD)
    )
    positions = (ctx * count + jnp.arange(count, dtype=jnp.int32)).astype(F32)
    angles = positions[:, None] * frequency[None, :]
    cosine = jnp.cos(angles)
    sine = jnp.where(lane % HEAD < HEAD // 2, -1.0, 1.0)[None, :] * jnp.sin(angles)

    gains = jnp.concatenate([gain_attn, gain_mlp])
    gain_rows = jnp.zeros((16, 2 * kvw), BF16).at[0, : 2 * rows].set(gains)
    kv_own = jnp.concatenate([jnp.concatenate([w_key, w_value], axis=1), gain_rows], axis=0)
    kv_weights = gather(kv_own)
    q_weights = gather(after(w_query, kv_weights[2]))
    out_weights = gather(after(w_out, q_weights[2]))
    stacked = jnp.stack([piece[rows, : 2 * rows] for piece in kv_weights]).astype(F32)
    owner = jnp.arange(n_shard, dtype=jnp.int32)[:, None] == (
        jnp.arange(n_shard, dtype=jnp.int32)[None, :] ^ shard
    )
    gains_full = jnp.sum(jnp.where(owner[:, :, None], stacked[None], 0.0), axis=1)
    gain_one = gains_full[:, :rows].reshape(1, width)
    gain_two = gains_full[:, rows:].reshape(1, width)

    hidden, kv = pl.pallas_call(
        functools.partial(keys_kernel, rows=rows, kvw=kvw),
        out_shape=(
            jax.ShapeDtypeStruct((count, width), BF16),
            jax.ShapeDtypeStruct((count, 2 * kvw), BF16),
        ),
        in_specs=[SMEM_SPEC] + [VMEM_SPEC] * (4 + n_shard),
        out_specs=(VMEM_SPEC, VMEM_SPEC),
        scratch_shapes=[pltpu.VMEM((width, 2 * kvw), BF16)],
        compiler_params=params(),
        cost_estimate=cost(4 * count * width * kvw, 8e6),
        name="keys",
    )(shard_arr, x, gain_one, cosine, sine, *kv_weights)
    all_kv = collect(kv)

    queries = pl.pallas_call(
        functools.partial(queries_kernel, rows=rows),
        out_shape=jax.ShapeDtypeStruct((count, qw), BF16),
        in_specs=[SMEM_SPEC] + [VMEM_SPEC] * (3 + n_shard),
        out_specs=VMEM_SPEC,
        scratch_shapes=[pltpu.VMEM((width, qw), BF16)],
        compiler_params=params(),
        cost_estimate=cost(2 * count * width * qw, 8e6),
        name="queries",
    )(shard_arr, hidden, cosine, sine, *q_weights)

    def columns(peer):
        start = peer * ff_own
        return jnp.concatenate(
            [
                lax.dynamic_slice_in_dim(w_gate, start, ff_own, 1),
                lax.dynamic_slice_in_dim(w_up, start, ff_own, 1),
            ],
            axis=1,
        )

    parts = [columns(shard)]
    done = out_weights[2]
    for distance in range(1, n_shard):
        parts.append(hop(after(columns(shard ^ distance), done), distance))
    gate_mat = jnp.zeros((width, ff_own), BF16)
    up_mat = jnp.zeros((width, ff_own), BF16)
    for distance, part in enumerate(parts):
        start = (shard ^ distance) * rows
        gate_mat = lax.dynamic_update_slice_in_dim(gate_mat, part[:, :ff_own], start, 0)
        up_mat = lax.dynamic_update_slice_in_dim(up_mat, part[:, ff_own:], start, 0)
    all_cot = jnp.concatenate(gather(after(cot, parts[3])), axis=0)

    blocks = n_ctx
    shared = dict(rows=rows, groups=groups, per=per, blocks=blocks)
    fixed = lambda *shape: pl.BlockSpec(shape, lambda step, table: (0,) * len(shape))
    kv_spec = pl.BlockSpec(
        (count, 2 * kvw), lambda step, table: (table[jnp.minimum(step, table[blocks])], 0)
    )
    once = lambda *shape: pl.BlockSpec(
        shape, lambda step, table: (0,) * len(shape), pipeline_mode=pl.Buffered(1)
    )
    weight_specs = [once(rows, width)] * n_shard
    out32, attended, log_total, mid, normed = pl.pallas_call(
        functools.partial(attend_kernel, **shared),
        out_shape=(
            jax.ShapeDtypeStruct((count, qw), F32),
            jax.ShapeDtypeStruct((count, qw), BF16),
            jax.ShapeDtypeStruct((8, per * count), F32),
            jax.ShapeDtypeStruct((count, width), F32),
            jax.ShapeDtypeStruct((count, width), BF16),
        ),
        grid_spec=pltpu.PrefetchScalarGridSpec(
            num_scalar_prefetch=1,
            grid=(blocks,),
            in_specs=[once(count, qw), kv_spec, once(count, width), once(1, width)]
            + weight_specs,
            out_specs=[
                fixed(count, qw),
                fixed(count, qw),
                fixed(8, per * count),
                fixed(count, width),
                fixed(count, width),
            ],
            scratch_shapes=[
                pltpu.VMEM((groups, HEAD, per * count), BF16),
                pltpu.VMEM((groups, HEAD, per * count), F32),
                pltpu.VMEM((8, per * count), F32),
                pltpu.VMEM((8, per * count), F32),
                pltpu.VMEM((qw, width), BF16),
            ],
        ),
        compiler_params=params(),
        cost_estimate=cost(4 * count * count * blocks * qw, 12e6, count * count * blocks * groups * per),
        name="attend",
    )(table, queries, all_kv, x, gain_two, *out_weights)

    all_normed = jnp.concatenate(gather(normed), axis=0)
    gate = nn(all_normed, gate_mat)
    up = nn(all_normed, up_mat)
    activated = (jax.nn.silu(gate) * up).astype(BF16)
    grad_down = tn(activated, all_cot).astype(BF16)
    grad_activated = nt(all_cot, w_down)
    sigmoid = jax.nn.sigmoid(gate)
    grad_gate = (grad_activated * up * (sigmoid * (1.0 + gate * (1.0 - sigmoid)))).astype(BF16)
    grad_up = (grad_activated * (gate * sigmoid)).astype(BF16)
    part_normed = (nt(grad_gate, gate_mat) + nt(grad_up, up_mat)).astype(BF16)
    grad_normed = reduce([part_normed[k * count : (k + 1) * count] for k in range(n_shard)])
    part_out = nn(activated, w_down).astype(BF16)
    part_out = after(part_out, grad_normed)
    output = (mid + reduce([part_out[k * count : (k + 1) * count] for k in range(n_shard)])).astype(
        BF16
    )[None]

    per_shard = n_ctx // n_shard
    tile = ff_own // per_shard

    def tiles(grad):
        cut = grad.astype(BF16).reshape(n_shard, rows, per_shard, tile).transpose(0, 2, 1, 3)
        return jnp.roll(cut, shard, axis=0).reshape(n_ctx, rows, tile)

    grad_gate_mat = tiles(tn(all_normed, grad_gate))
    grad_up_mat = tiles(tn(all_normed, grad_up))
    down_rows = ff_own // n_ctx
    splits = 3
    down_tiles = (
        grad_down.reshape(n_ctx, down_rows, splits, width // splits)
        .transpose(0, 2, 1, 3)
        .reshape(n_ctx, splits * down_rows, width // splits)
    )
    gate_up = scatter(jnp.concatenate([grad_gate_mat, grad_up_mat], axis=1))
    pairs = []
    for index in range(n_ctx):
        for source in range(n_shard):
            target = (places[index] // per_shard - source) % n_shard
            pairs.append((index * n_shard + source, index * n_shard + target))
    gate_up = lax.ppermute(gate_up, ("ctx", "shard"), pairs)
    down_sum = collect(scatter(down_tiles)[None])
    gate_up = collect(gate_up[None])

    def untile(part):
        back = jnp.roll(part.reshape(n_shard, per_shard, rows, tile), -shard, axis=0)
        return back.reshape(n_ctx, rows, tile).transpose(1, 0, 2).reshape(rows, ff).astype(F32)

    grad_w_gate = untile(gate_up[:, :rows])
    grad_w_up = untile(gate_up[:, rows:])
    grad_w_down = (
        down_sum.reshape(n_ctx, splits, down_rows, width // splits)
        .transpose(0, 2, 1, 3)
        .reshape(ff_own, width)
        .astype(F32)
    )

    place_spec = pl.BlockSpec((count, 2 * kvw), lambda step, table: (table[step], 0))
    grad_query, grad_kv, branch, grad_mid, gain_two_part = pl.pallas_call(
        functools.partial(attend_back_kernel, **shared),
        out_shape=(
            jax.ShapeDtypeStruct((count, qw), BF16),
            jax.ShapeDtypeStruct((blocks * count, 2 * kvw), BF16),
            jax.ShapeDtypeStruct((count, width), BF16),
            jax.ShapeDtypeStruct((count, width), F32),
            jax.ShapeDtypeStruct((1, width), F32),
        ),
        grid_spec=pltpu.PrefetchScalarGridSpec(
            num_scalar_prefetch=1,
            grid=(blocks,),
            in_specs=[
                once(count, qw),
                kv_spec,
                once(count, qw),
                once(8, per * count),
                once(count, width),
                once(1, width),
                once(count, width),
                once(count, width),
                once(count, LANES),
                once(count, LANES),
            ]
            + weight_specs,
            out_specs=[
                fixed(count, qw),
                place_spec,
                fixed(count, width),
                fixed(count, width),
                fixed(1, width),
            ],
            scratch_shapes=[
                pltpu.VMEM((qw, width), BF16),
                pltpu.VMEM((groups, per * count, HEAD), BF16),
                pltpu.VMEM((groups, HEAD, per * count), BF16),
                pltpu.VMEM((groups, per * count, HEAD), BF16),
                pltpu.VMEM((groups, HEAD, per * count), BF16),
                pltpu.VMEM((8, per * count), F32),
                pltpu.VMEM((groups, HEAD, per * count), F32),
                pltpu.VMEM((count, qw), F32),
            ],
        ),
        compiler_params=params(),
        cost_estimate=cost(10 * count * count * blocks * qw, 14e6, count * count * blocks * groups * per),
        name="attend_back",
    )(
        table,
        queries,
        all_kv,
        out32,
        log_total,
        mid,
        gain_two,
        cot,
        grad_normed,
        cosine,
        sine,
        *out_weights,
    )
    own_kv = scatter(grad_kv.reshape(n_ctx, count, 2 * kvw))

    def weight_grad(left, right, name):
        columns_out = right.shape[1]
        return pl.pallas_call(
            functools.partial(weight_grad_kernel, rows=rows),
            out_shape=(jax.ShapeDtypeStruct((rows, columns_out), BF16),) * n_shard,
            in_specs=[SMEM_SPEC, VMEM_SPEC, VMEM_SPEC],
            out_specs=(VMEM_SPEC,) * n_shard,
            scratch_shapes=[pltpu.VMEM((left.shape[1], columns_out), F32)],
            compiler_params=params(),
            cost_estimate=cost(2 * count * left.shape[1] * columns_out, 8e6),
            name=name,
        )(shard_arr, left, right)

    sum_out = reduce(weight_grad(attended, branch, "grad_out"))
    sum_query = reduce(weight_grad(hidden, grad_query, "grad_query"))

    grad_kv_pre = pl.pallas_call(
        functools.partial(unturn_kernel, kvw=kvw),
        out_shape=jax.ShapeDtypeStruct((count, 2 * kvw), BF16),
        in_specs=[VMEM_SPEC] * 3,
        out_specs=VMEM_SPEC,
        compiler_params=params(),
        cost_estimate=cost(4 * count * kvw, 1e6),
        name="unturn",
    )(own_kv, cosine, sine)
    sum_kv = reduce(weight_grad(hidden, grad_kv_pre, "grad_kv"))

    merged = jnp.concatenate([sum_query, sum_out, sum_kv], axis=1).astype(BF16)
    span = merged.shape[1] // n_ctx
    merged = merged.reshape(rows, n_ctx, span).transpose(1, 0, 2)
    merged = collect(scatter(merged)[None])
    merged = merged.transpose(1, 0, 2).reshape(rows, 2 * qw + 2 * kvw)
    grad_w_query = merged[:, :qw].astype(F32)
    grad_w_out = merged[:, qw : 2 * qw].astype(F32)
    grad_w_key = merged[:, 2 * qw : 2 * qw + kvw].astype(F32)
    grad_w_value = merged[:, 2 * qw + kvw :].astype(F32)

    grad_x, gain_one_part = pl.pallas_call(
        functools.partial(inputs_kernel, rows=rows, hops=n_shard),
        out_shape=(
            jax.ShapeDtypeStruct((count, width), BF16),
            jax.ShapeDtypeStruct((1, width), F32),
        ),
        in_specs=[SMEM_SPEC] + [VMEM_SPEC] * (5 + 2 * n_shard),
        out_specs=(VMEM_SPEC, VMEM_SPEC),
        scratch_shapes=[pltpu.VMEM((width, qw), BF16), pltpu.VMEM((width, 2 * kvw), BF16)],
        compiler_params=params(),
        cost_estimate=cost(2 * count * width * (qw + 2 * kvw), 12e6),
        name="grad_inputs",
    )(shard_arr, grad_query, grad_kv_pre, x, gain_one, grad_mid, *q_weights, *kv_weights)

    gain_parts = jnp.concatenate([gain_one_part, gain_two_part], axis=0)
    distance = 1
    while distance < n_shard:
        gain_parts = gain_parts + hop(gain_parts, distance)
        distance *= 2
    distance = 1
    while distance < n_ctx:
        gain_parts = gain_parts + lax.ppermute(
            gain_parts, "ctx", [(index, index ^ distance) for index in range(n_ctx)]
        )
        distance *= 2
    own_gains = lax.dynamic_slice_in_dim(gain_parts, shard * rows, rows, 1)

    return (
        output,
        grad_x[None],
        own_gains[0],
        grad_w_query,
        grad_w_key,
        grad_w_value,
        grad_w_out,
        own_gains[1],
        grad_w_gate,
        grad_w_up,
        grad_w_down,
    )


def solution(mesh):
    tokens = P("shard", "ctx", None)
    split = P("shard", None)
    gain = P("shard")
    placed = (tokens, gain, split, split, split, split, gain, split, split, split, tokens)
    return jax.shard_map(
        functools.partial(on_device, n_ctx=mesh.shape["ctx"], n_shard=mesh.shape["shard"]),
        mesh=mesh,
        in_specs=placed,
        out_specs=(tokens, tokens, gain, split, split, split, split, gain, split, split, split),
        check_vma=False,
    )
```

time: 1480 us -> 529 us (0.36)
  the two profiles are of different devices: /device:TPU:9 before, /device:TPU:0 now
where the time goes in v1:
time: 529 us; the launch traced here: 520 us
  waiting for transfers between devices  282 us (53%)
  local copies, waits for them, and re-layouts  80.4 us (15%)
  starting transfers between devices  39.8 us (8%)
  Pallas kernels  39.5 us (7%)
  matrix products  37.9 us (7%)
  other arithmetic  25.2 us (5%)
  between operations  15.3 us (3%)
    ppermute x35, waiting for transfers between devices, hop(): return lax.ppermute(value, 'shard', pairs)  115 us
    reduce_scatter x4, waiting for transfers between devices, scatter(): lax.psum_scatter(value, 'ctx', scatter_dimension=0, axis_index_groups=[or...  87.2 us
    all_gather x4, waiting for transfers between devices, collect(): lax.all_gather(value, 'ctx', axis=0, axis_index_groups=[order], tiled=True)  78 us
    unnamed x138, local copies, waits for them, and re-layouts  34.6 us
    ppermute x35, starting transfers between devices, hop(): return lax.ppermute(value, 'shard', pairs)  26.5 us
    dot_general x3, matrix products, tn(): lax.dot_general(left, right, (((0,), (0,)), ((), ())), preferred_element_...  15.8 us
    pallas_call x1, Pallas kernels, on_device(): pl.pallas_call(functools.partial(attend_back_kernel, **shared), out_shape...  15.1 us
    reshape x4, local copies, waits for them, and re-layouts, tiles(): grad.astype(BF16).reshape(n_shard, rows, per_shard, tile)  13.9 us
  transfers between devices with their start and end apart: 47, of which 25 were waited for; matrix products, arithmetic and copies ran while one was open for 18% of the time, Pallas kernels for 4%

profile of v1, /device:TPU:0, one launch (start us, length us, event | category | flops | bytes accessed | tf_op | source)
XLA Modules:
  0.0 520.0 jit_solution(17810869367897654780)
XLA Ops:
  9.2 3.0 collective-permute-start.1
  12.3 10.8 %collective-permute-done.1.rest_2_.rest_6_ = bf16[304,768]{1,0:T(8,128)(2,1)} collective-permute-done((bf16[304,768]{1,0:T(8,128)(2,1)S(1)}, bf16[304,768]{1,0:T(8,128)(2,1)}, u32[]{:S(2)}, u32[]{:S(2)}) %collective-permute-start.1) | collective-permute-done | bytes 466976 | tf_op jit(solution)/shard_map/ppermute | solution.py:344
  28.3 2.9 keys.1
  32.0 1.8 collective-permute-start.4
  33.8 15.7 %collective-permute-done.4.rest_2_ = bf16[288,1152]{1,0:T(8,128)(2,1)} collective-permute-done((bf16[288,1152]{1,0:T(8,128)(2,1)S(1)}, bf16[288,1152]{1,0:T(8,128)(2,1)}, u32[]{:S(2)}, u32[]{:S(2)}) %collective-permute-start.4) | collective-permute-done | bytes 663584 | tf_op jit(solution)/shard_map/ppermute | solution.py:344
  49.5 1.7 collective-permute-start.7
  57.2 9.2 %collective-permute-done.7.rest_2_ = bf16[288,1152]{1,0:T(8,128)(2,1)} collective-permute-done((bf16[288,1152]{1,0:T(8,128)(2,1)}, bf16[288,1152]{1,0:T(8,128)(2,1)}, u32[]{:S(2)}, u32[]{:S(2)}) %collective-permute-start.7) | collective-permute-done | bytes 663584 | tf_op jit(solution)/shard_map/ppermute | solution.py:344
  67.9 1.7 collective-permute-start.12
  70.5 3.0 collective-permute-done.3.rest_1_
  75.3 3.0 queries.1.q_ref
  78.3 10.0 %collective-permute-done.14 = bf16[288,1536]{1,0:T(8,128)(2,1)} collective-permute-done((bf16[288,1536]{1,0:T(8,128)(2,1)}, bf16[288,1536]{1,0:T(8,128)(2,1)}, u32[]{:S(2)}, u32[]{:S(2)}) %collective-permute-start.14) | collective-permute-done | bytes 884768 | tf_op jit(solution)/shard_map/ppermute | solution.py:344
  88.4 2.0 collective-permute-start.16
  90.4 2.0 slice_dynamic-update-slice_fusion.5
  92.4 15.5 %collective-permute-done.13 = bf16[288,1536]{1,0:T(8,128)(2,1)} collective-permute-done((bf16[288,1536]{1,0:T(8,128)(2,1)}, bf16[288,1536]{1,0:T(8,128)(2,1)}, u32[]{:S(2)}, u32[]{:S(2)}) %collective-permute-start.13) | collective-permute-done | bytes 884768 | tf_op jit(solution)/shard_map/ppermute | solution.py:344
  107.9 2.0 slice_dynamic-update-slice_fusion.4
  109.9 2.0 slice_dynamic-update-slice_fusion.3
  111.9 8.4 %collective-permute-done.16 = bf16[256,1152]{1,0:T(8,128)(2,1)} collective-permute-done((bf16[256,1152]{1,0:T(8,128)(2,1)S(1)}, bf16[256,1152]{1,0:T(8,128)(2,1)}, u32[]{:S(2)}, u32[]{:S(2)}) %collective-permute-start.16) | collective-permute-done | bytes 589856 | tf_op jit(solution)/shard_map/ppermute | solution.py:344
  129.0 8.6 %attend.1 = (f32[256,1152]{1,0:T(8,128)S(1)}, bf16[256,1152]{1,0:T(8,128)(2,1)S(1)}, f32[8,768]{1,0:T(8,128)S(1)}, f32[256,1152]{1,0:T(8,128)S(1)}, bf16[256,1152]{1,0:T(8,128)(2,1)S(1)}) custom-call(s32[10]{0:T(128)S(1)} %pad_add_fusion.table_ref, bf16[256,1152]{1,0:T(8,128)(2,1)S(1)} %copy-done.33, bf16[2048,768]{1,0:T(8,128)(2,1)} %all-gather.6.cloned.1.call-done.kv_ref, ...), custom_call_target="tpu_custom_call" | custom-call | flops 2415919104 | bytes 12000000 | tf_op jit(solution)/shard_map/attend/pallas_call | solution.py:450
  139.9 2.2 fusion.19
  142.1 11.3 %collective-permute-done.10 = bf16[256,1152]{1,0:T(8,128)(2,1)S(1)} collective-permute-done((bf16[256,1152]{1,0:T(8,128)(2,1)S(1)}, bf16[256,1152]{1,0:T(8,128)(2,1)S(1)}, u32[]{:S(2)}, u32[]{:S(2)}) %collective-permute-start.10) | collective-permute-done | bytes 589856 | tf_op jit(solution)/shard_map/ppermute | solution.py:344
  153.6 1.8 collective-permute-done.11
  155.5 4.6 fusion.18
  160.1 4.5 multiply_convert_fusion.1
  164.6 4.9 fusion.20
  169.5 2.3 add_convert_fusion
  174.8 14.8 %collective-permute-done.20 = bf16[256,1152]{1,0:T(8,128)(2,1)S(1)} collective-permute-done((bf16[256,1152]{1,0:T(8,128)(2,1)S(1)}, bf16[256,1152]{1,0:T(8,128)(2,1)S(1)}, u32[]{:S(2)}, u32[]{:S(2)}) %collective-permute-start.20) | collective-permute-done | bytes 589856 | tf_op jit(solution)/shard_map/ppermute | solution.py:344
  189.9 15.1 %attend_back.1 = (bf16[256,1152]{1,0:T(8,128)(2,1)S(1)}, bf16[2048,768]{1,0:T(8,128)(2,1)}, bf16[256,1152]{1,0:T(8,128)(2,1)S(1)}, f32[256,1152]{1,0:T(8,128)S(1)}, f32[1,1152]{1,0:T(1,128)S(1)}) custom-call(s32[10]{0:T(128)S(1)} %pad_add_fusion.table_ref, bf16[256,1152]{1,0:T(8,128)(2,1)S(1)} %copy-done.34, ...), custom_call_target="tpu_custom_call" | custom-call | flops 6039797760 | bytes 14000000 | tf_op jit(solution)/shard_map/attend_back/pallas_call | solution.py:541
  207.7 5.7 %convolution_convert_fusion.1 = bf16[768,1152]{1,0:T(8,128)(2,1)} fusion(bf16[1024,768]{1,0:T(8,128)(2,1)} %get-tuple-element.138, bf16[1024,1152]{1,0:T(8,128)(2,1)} %copy-done.58), kind=kOutput, calls=%fused_computation.12 | convolution fusion | flops 1812824064 | bytes 5701632 | tf_op jit(solution)/shard_map/dot_general | solution.py:31
  213.4 4.0 copy.56
  217.4 5.1 reshape.199
  222.5 4.2 copy.57
  226.8 5.4 %convolution_convert_fusion.2 = bf16[1152,768]{1,0:T(8,128)(2,1)} fusion(bf16[1024,1152]{1,0:T(8,128)(2,1)} %copy-done.59, bf16[1024,768]{1,0:T(8,128)(2,1)} %copy-done.63), kind=kOutput, calls=%fused_computation.13 | convolution fusion | flops 1812824064 | bytes 5701632 | tf_op jit(solution)/shard_map/dot_general | solution.py:31
  232.2 4.5 reshape.195
  236.7 3.1 copy.73
  239.7 4.7 convolution_convert_fusion.3
  244.4 4.5 reshape.193
  249.0 1.8 copy.74
  252.5 2.2 pad_maximum_fusion
  256.8 2.1 grad_query.1
  259.8 2.1 grad_out.1
  266.7 18.9 %reduce-scatter.5.cloned.1.call-done = bf16[1,256,768]{2,1,0:T(8,128)(2,1)} async-done(((bf16[8,256,768]{2,1,0:T(8,128)(2,1)}), bf16[1,256,768]{2,1,0:T(8,128)(2,1)}) %reduce-scatter.5.cloned.1.call-update) | async-done | bytes 393232 | tf_op jit(solution)/shard_map/reduce_scatter | solution.py:362
  296.8 8.4 %collective-permute-done.37 = bf16[288,768]{1,0:T(8,128)(2,1)S(1)} collective-permute-done((bf16[288,768]{1,0:T(8,128)(2,1)S(1)}, bf16[288,768]{1,0:T(8,128)(2,1)S(1)}, u32[]{:S(2)}, u32[]{:S(2)}) %collective-permute-start.37) | collective-permute-done | bytes 442400 | tf_op jit(solution)/shard_map/ppermute | solution.py:344
  307.1 12.6 %reduce-scatter.11.cloned.1.call-done = bf16[1,288,384]{2,1,0:T(8,128)(2,1)} async-done(((bf16[8,288,384]{2,1,0:T(8,128)(2,1)}), bf16[1,288,384]{2,1,0:T(8,128)(2,1)}) %reduce-scatter.11.cloned.1.call-update) | async-done | bytes 221200 | tf_op jit(solution)/shard_map/reduce_scatter | solution.py:362
  319.7 44.2 %reduce-scatter.9.cloned.1.call-done = bf16[1,576,384]{2,1,0:T(8,128)(2,1)} async-done(((bf16[8,576,384]{2,1,0:T(8,128)(2,1)}), bf16[1,576,384]{2,1,0:T(8,128)(2,1)}) %reduce-scatter.9.cloned.1.call-update) | async-done | bytes 442384 | tf_op jit(solution)/shard_map/reduce_scatter | solution.py:362
  363.9 5.0 collective-permute-start.38
  369.2 3.7 convolution_convert_fusion
  373.8 4.2 collective-permute-start.22
  378.1 4.7 grad_inputs.1
  382.8 1.7 collective-permute-start.24
  386.9 11.5 %reduce-scatter.7.cloned.1.call-done = bf16[1,288,384]{2,1,0:T(8,128)(2,1)} async-done(((bf16[8,288,384]{2,1,0:T(8,128)(2,1)}), bf16[1,288,384]{2,1,0:T(8,128)(2,1)}) %reduce-scatter.7.cloned.1.call-update) | async-done | bytes 221200 | tf_op jit(solution)/shard_map/reduce_scatter | solution.py:362
  400.1 2.2 collective-permute-done.25
  402.3 6.2 %collective-permute-start.26 = (f32[2,1152]{1,0:T(2,128)S(1)}, f32[2,1152]{1,0:T(2,128)S(1)}, u32[]{:S(2)}, u32[]{:S(2)}) collective-permute-start(f32[2,1152]{1,0:T(2,128)S(1)} %fusion.39), channel_id=1, source_target_pairs={{0,4},{4,0},{8,12},{12,8},{16,20},{20,16},{24,28},{28,24},{1,5},{5... | collective-permute-start | bytes 27656 | tf_op jit(solution)/shard_map/ppermute | solution.py:661
  411.5 2.5 fusion.6
  414.1 17.7 %all-gather.10.cloned.1.call-done = bf16[8,288,384]{2,1,0:T(8,128)(2,1)} async-done(((bf16[1,288,384]{2,1,0:T(8,128)(2,1)}), bf16[8,288,384]{2,1,0:T(8,128)(2,1)}) %all-gather.10.cloned.1.call-update) | async-done | bytes 1769488 | tf_op jit(solution)/shard_map/all_gather | solution.py:367
  431.8 1.9 convert_bitcast_fusion
  433.7 2.4 copy.60
  436.1 2.0 copy.66
  438.9 35.4 %all-gather.12.cloned.1.call-done = bf16[4608,384]{1,0:T(8,128)(2,1)} async-done(((bf16[576,384]{1,0:T(8,128)(2,1)}), bf16[4608,384]{1,0:T(8,128)(2,1)}) %all-gather.12.cloned.1.call-update) | async-done | bytes 3538960 | tf_op jit(solution)/shard_map/all_gather | solution.py:367
  474.3 2.4 fusion.14
  477.8 2.2 copy.64
  481.2 2.2 copy.65
  483.4 24.9 %all-gather.8.cloned.1.call-done = bf16[8,288,384]{2,1,0:T(8,128)(2,1)} async-done(((bf16[1,288,384]{2,1,0:T(8,128)(2,1)}), bf16[8,288,384]{2,1,0:T(8,128)(2,1)}) %all-gather.8.cloned.1.call-update) | async-done | bytes 1769488 | tf_op jit(solution)/shard_map/all_gather | solution.py:367
  508.4 1.8 copy.63
  511.1 1.7 slice_convert_fusion
  (262 shorter events, 70.2 us)
Async XLA Ops:
  7.2 132.7 %copy-start = (bf16[768,1152]{1,0:T(8,128)(2,1)S(1)}, bf16[768,1152]{1,0:T(8,128)(2,1)}, u32[]{:S(2)}) copy-start(bf16[768,1152]{1,0:T(8,128)(2,1)} %param.25) | copy-start | bytes 5308420
  7.2 117.4 %all-gather.6.cloned.1.call-start = ((), (), s32[]{:S(2)}) async-start(), calls=%async_computation.4 | async-start | bytes 3538944 | tf_op jit(solution)/shard_map/all_gather | solution.py:367
  9.2 22.8 %copy-start.1 = (bf16[288,1152]{1,0:T(8,128)(2,1)S(1)}, bf16[288,1152]{1,0:T(8,128)(2,1)}, u32[]{:S(2)}) copy-start(bf16[288,1152]{1,0:T(8,128)(2,1)} %rest_0_.3) | copy-start | bytes 1990660
  9.2 13.8 %collective-permute-start.1 = (bf16[304,768]{1,0:T(8,128)(2,1)S(1)}, bf16[304,768]{1,0:T(8,128)(2,1)}, u32[]{:S(2)}, u32[]{:S(2)}) collective-permute-start(bf16[304,768]{1,0:T(8,128)(2,1)S(1)} %fusion.7.rest_0_.rest_4_), channel_id=1, source_target_pairs={{0,2},{1,3},{2,0},{3,1},{4,6},{5,7},{6,4},{7,5},{8,10},{9,11},{10,... | collective-permute-start | bytes 1400840 | tf_op jit(solution)/shard_map/ppermute | solution.py:344
  12.2 12.1 %collective-permute-start = (bf16[304,768]{1,0:T(8,128)(2,1)S(1)}, bf16[304,768]{1,0:T(8,128)(2,1)}, u32[]{:S(2)}, u32[]{:S(2)}) collective-permute-start(bf16[304,768]{1,0:T(8,128)(2,1)S(1)} %fusion.7.rest_0_.rest_4_), channel_id=1, source_target_pairs={{0,1},{1,0},{2,3},{3,2},{4,5},{5,4},{6,7},{7,6},{8,9},{9,8},{10,11... | collective-permute-start | bytes 1400840 | tf_op jit(solution)/shard_map/ppermute | solution.py:344
  23.0 2.0 collective-permute-start.2
  23.6 50.6 %copy-start.4 = (f32[256,128]{1,0:T(8,128)}, f32[256,128]{1,0:T(8,128)S(1)}, u32[]{:S(2)}) copy-start(f32[256,128]{1,0:T(8,128)S(1)} %get-tuple-element.165.sin_ref) | copy-start | bytes 393220
  23.6 50.6 %copy-start.7 = (f32[256,128]{1,0:T(8,128)}, f32[256,128]{1,0:T(8,128)S(1)}, u32[]{:S(2)}) copy-start(f32[256,128]{1,0:T(8,128)S(1)} %get-tuple-element.166.cos_ref) | copy-start | bytes 393220
  32.0 253.7 %reduce-scatter.5.cloned.1.call-start = ((), (), s32[]{:S(2)}) async-start(), calls=%async_computation.5 | async-start | bytes 3538944 | tf_op jit(solution)/shard_map/reduce_scatter | solution.py:362
  32.0 17.5 %collective-permute-start.4 = (bf16[288,1152]{1,0:T(8,128)(2,1)S(1)}, bf16[288,1152]{1,0:T(8,128)(2,1)}, u32[]{:S(2)}, u32[]{:S(2)}) collective-permute-start(bf16[288,1152]{1,0:T(8,128)(2,1)S(1)} %copy-done.1), channel_id=1, source_target_pairs={{0,2},{1,3},{2,0},{3,1},{4,6},{5,7},{6,4},{7,5},{8,10},{9,11},{10,... | collective-permute-start | bytes 1990664 | tf_op jit(solution)/shard_map/ppermute | solution.py:344
  49.5 16.9 %collective-permute-start.7 = (bf16[288,1152]{1,0:T(8,128)(2,1)}, bf16[288,1152]{1,0:T(8,128)(2,1)}, u32[]{:S(2)}, u32[]{:S(2)}) collective-permute-start(bf16[288,1152]{1,0:T(8,128)(2,1)} %rest_0_.2), channel_id=1, source_target_pairs={{0,2},{1,3},{2,0},{3,1},{4,6},{5,7},{6,4},{7,5},{8,10},{9,11},{10,... | collective-permute-start | bytes 1990664 | tf_op jit(solution)/shard_map/ppermute | solution.py:344
  66.4 22.0 %collective-permute-start.14 = (bf16[288,1536]{1,0:T(8,128)(2,1)}, bf16[288,1536]{1,0:T(8,128)(2,1)}, u32[]{:S(2)}, u32[]{:S(2)}) collective-permute-start(bf16[288,1536]{1,0:T(8,128)(2,1)} %pad_maximum_fusion.4), channel_id=1, source_target_pairs={{0,3},{1,2},{2,1},{3,0},{4,7},{5,6},{6,5},{7,4},{8,11},{9,10},{10,... | collective-permute-start | bytes 2654216 | tf_op jit(solution)/shard_map/ppermute | solution.py:344
  67.9 22.5 %collective-permute-start.12 = (bf16[288,1536]{1,0:T(8,128)(2,1)}, bf16[288,1536]{1,0:T(8,128)(2,1)}, u32[]{:S(2)}, u32[]{:S(2)}) collective-permute-start(bf16[288,1536]{1,0:T(8,128)(2,1)} %get-tuple-element.63), channel_id=1, source_target_pairs={{0,1},{1,0},{2,3},{3,2},{4,5},{5,4},{6,7},{7,6},{8,9},{9,8},{10,11... | collective-permute-start | bytes 2654216 | tf_op jit(solution)/shard_map/ppermute | solution.py:344
  69.6 3.9 collective-permute-start.3
  69.6 4.3 collective-permute-start.5
  70.1 37.8 %collective-permute-start.13 = (bf16[288,1536]{1,0:T(8,128)(2,1)}, bf16[288,1536]{1,0:T(8,128)(2,1)}, u32[]{:S(2)}, u32[]{:S(2)}) collective-permute-start(bf16[288,1536]{1,0:T(8,128)(2,1)} %get-tuple-element.64), channel_id=1, source_target_pairs={{0,2},{1,3},{2,0},{3,1},{4,6},{5,7},{6,4},{7,5},{8,10},{9,11},{10,... | collective-permute-start | bytes 2654216 | tf_op jit(solution)/shard_map/ppermute | solution.py:344
  73.5 48.0 %collective-permute-start.6 = (bf16[288,1152]{1,0:T(8,128)(2,1)}, bf16[288,1152]{1,0:T(8,128)(2,1)S(1)}, u32[]{:S(2)}, u32[]{:S(2)}) collective-permute-start(bf16[288,1152]{1,0:T(8,128)(2,1)} %rest_0_.2), channel_id=1, source_target_pairs={{0,1},{1,0},{2,3},{3,2},{4,5},{5,4},{6,7},{7,6},{8,9},{9,8},{10,11... | collective-permute-start | bytes 1990664 | tf_op jit(solution)/shard_map/ppermute | solution.py:344
  73.9 49.9 %collective-permute-start.8 = (bf16[288,1152]{1,0:T(8,128)(2,1)}, bf16[288,1152]{1,0:T(8,128)(2,1)S(1)}, u32[]{:S(2)}, u32[]{:S(2)}) collective-permute-start(bf16[288,1152]{1,0:T(8,128)(2,1)} %collective-permute-done.7.rest_2_), channel_id=1, source_target_pairs={{0,1},{1,0},{2,3},{3,2},{4,5},{5,4},{6,7},{7,6},{8,9},{9,8},{10,11... | collective-permute-start | bytes 1990664 | tf_op jit(solution)/shard_map/ppermute | solution.py:344
  75.3 13.1 %copy-start.26 = (bf16[1,256,1152]{2,1,0:T(8,128)(2,1)S(1)}, bf16[1,256,1152]{2,1,0:T(8,128)(2,1)}, u32[]{:S(2)}) copy-start(bf16[1,256,1152]{2,1,0:T(8,128)(2,1)} %param.26) | copy-start | bytes 1769476
  75.3 15.1 %copy-start.53 = (bf16[1152,768]{1,0:T(8,128)(2,1)S(1)}, bf16[1152,768]{1,0:T(8,128)(2,1)}, u32[]{:S(2)}) copy-start(bf16[1152,768]{1,0:T(8,128)(2,1)} %copy-done.52) | copy-start | bytes 5308420
  78.3 31.6 %copy-start.32 = (bf16[256,1152]{1,0:T(8,128)(2,1)}, bf16[256,1152]{1,0:T(8,128)(2,1)S(1)}, u32[]{:S(2)}) copy-start(bf16[256,1152]{1,0:T(8,128)(2,1)S(1)} %queries.1.q_ref) | copy-start | bytes 1769476
  88.4 31.9 %collective-permute-start.16 = (bf16[256,1152]{1,0:T(8,128)(2,1)S(1)}, bf16[256,1152]{1,0:T(8,128)(2,1)}, u32[]{:S(2)}, u32[]{:S(2)}) collective-permute-start(bf16[256,1152]{1,0:T(8,128)(2,1)S(1)} %bitcast.77), channel_id=1, source_target_pairs={{0,2},{1,3},{2,0},{3,1},{4,6},{5,7},{6,4},{7,5},{8,10},{9,11},{10,... | collective-permute-start | bytes 1769480 | tf_op jit(solution)/shard_map/ppermute | solution.py:344
  90.4 29.9 %collective-permute-start.15 = (bf16[256,1152]{1,0:T(8,128)(2,1)S(1)}, bf16[256,1152]{1,0:T(8,128)(2,1)S(1)}, u32[]{:S(2)}, u32[]{:S(2)}) collective-permute-start(bf16[256,1152]{1,0:T(8,128)(2,1)S(1)} %bitcast.78), channel_id=1, source_target_pairs={{0,1},{1,0},{2,3},{3,2},{4,5},{5,4},{6,7},{7,6},{8,9},{9,8},{10,11... | collective-permute-start | bytes 1769480 | tf_op jit(solution)/shard_map/ppermute | solution.py:344
  111.8 12.8 %copy-start.3 = (bf16[1,256,1152]{2,1,0:T(8,128)(2,1)S(1)}, bf16[1,256,1152]{2,1,0:T(8,128)(2,1)}, u32[]{:S(2)}) copy-start(bf16[1,256,1152]{2,1,0:T(8,128)(2,1)} %param.16) | copy-start | bytes 1769476
  120.2 18.0 %collective-permute-start.17 = (bf16[256,1152]{1,0:T(8,128)(2,1)}, bf16[256,1152]{1,0:T(8,128)(2,1)}, u32[]{:S(2)}, u32[]{:S(2)}) collective-permute-start(bf16[256,1152]{1,0:T(8,128)(2,1)} %collective-permute-done.16), channel_id=1, source_target_pairs={{0,1},{1,0},{2,3},{3,2},{4,5},{5,4},{6,7},{7,6},{8,9},{9,8},{10,11... | collective-permute-start | bytes 1769480 | tf_op jit(solution)/shard_map/ppermute | solution.py:344
  137.6 52.2 %copy-start.15 = (f32[256,1152]{1,0:T(8,128)}, f32[256,1152]{1,0:T(8,128)S(1)}, u32[]{:S(2)}) copy-start(f32[256,1152]{1,0:T(8,128)S(1)} %get-tuple-element.61.mid_ref) | copy-start | bytes 3538948
  137.6 15.8 %collective-permute-start.10 = (bf16[256,1152]{1,0:T(8,128)(2,1)S(1)}, bf16[256,1152]{1,0:T(8,128)(2,1)S(1)}, u32[]{:S(2)}, u32[]{:S(2)}) collective-permute-start(bf16[256,1152]{1,0:T(8,128)(2,1)S(1)} %get-tuple-element.62), channel_id=1, source_target_pairs={{0,2},{1,3},{2,0},{3,1},{4,6},{5,7},{6,4},{7,5},{8,10},{9,11},{10,... | collective-permute-start | bytes 1769480 | tf_op jit(solution)/shard_map/ppermute | solution.py:344
  139.4 14.1 %collective-permute-start.9 = (bf16[256,1152]{1,0:T(8,128)(2,1)S(1)}, bf16[256,1152]{1,0:T(8,128)(2,1)S(1)}, u32[]{:S(2)}, u32[]{:S(2)}) collective-permute-start(bf16[256,1152]{1,0:T(8,128)(2,1)S(1)} %get-tuple-element.62), channel_id=1, source_target_pairs={{0,1},{1,0},{2,3},{3,2},{4,5},{5,4},{6,7},{7,6},{8,9},{9,8},{10,11... | collective-permute-start | bytes 1769480 | tf_op jit(solution)/shard_map/ppermute | solution.py:344
  153.4 2.0 collective-permute-start.11
  171.9 2.1 collective-permute-start.19
  172.1 2.7 collective-permute-start.18
  174.0 15.9 %copy-start.43 = (bf16[288,1152]{1,0:T(8,128)(2,1)S(1)}, bf16[288,1152]{1,0:T(8,128)(2,1)}, u32[]{:S(2)}) copy-start(bf16[288,1152]{1,0:T(8,128)(2,1)} %copy-done.41) | copy-start | bytes 1990660
  174.1 15.7 %copy-start.5 = (f32[256,128]{1,0:T(8,128)S(1)}, f32[256,128]{1,0:T(8,128)}, u32[]{:S(2)}) copy-start(f32[256,128]{1,0:T(8,128)} %copy-done.4) | copy-start | bytes 393220
  174.1 15.7 %copy-start.8 = (f32[256,128]{1,0:T(8,128)S(1)}, f32[256,128]{1,0:T(8,128)}, u32[]{:S(2)}) copy-start(f32[256,128]{1,0:T(8,128)} %copy-done.7) | copy-start | bytes 393220
  174.1 15.7 %copy-start.27 = (bf16[1,256,1152]{2,1,0:T(8,128)(2,1)S(1)}, bf16[1,256,1152]{2,1,0:T(8,128)(2,1)}, u32[]{:S(2)}) copy-start(bf16[1,256,1152]{2,1,0:T(8,128)(2,1)} %param.26) | copy-start | bytes 1769476
  174.2 15.7 %copy-start.34 = (bf16[256,1152]{1,0:T(8,128)(2,1)S(1)}, bf16[256,1152]{1,0:T(8,128)(2,1)}, u32[]{:S(2)}) copy-start(bf16[256,1152]{1,0:T(8,128)(2,1)} %copy-done.32) | copy-start | bytes 1769476
  174.2 15.7 %copy-start.37 = (bf16[288,1152]{1,0:T(8,128)(2,1)S(1)}, bf16[288,1152]{1,0:T(8,128)(2,1)}, u32[]{:S(2)}) copy-start(bf16[288,1152]{1,0:T(8,128)(2,1)} %rest_0_.2) | copy-start | bytes 1990660
  174.2 15.7 %copy-start.40 = (bf16[288,1152]{1,0:T(8,128)(2,1)S(1)}, bf16[288,1152]{1,0:T(8,128)(2,1)}, u32[]{:S(2)}) copy-start(bf16[288,1152]{1,0:T(8,128)(2,1)} %copy-done.38) | copy-start | bytes 1990660
  174.2 15.4 %collective-permute-start.20 = (bf16[256,1152]{1,0:T(8,128)(2,1)S(1)}, bf16[256,1152]{1,0:T(8,128)(2,1)S(1)}, u32[]{:S(2)}, u32[]{:S(2)}) collective-permute-start(bf16[256,1152]{1,0:T(8,128)(2,1)S(1)} %add_convert_fusion.7), channel_id=1, source_target_pairs={{0,2},{1,3},{2,0},{3,1},{4,6},{5,7},{6,4},{7,5},{8,10},{9,11},{10,... | collective-permute-start | bytes 1769480 | tf_op jit(solution)/shard_map/ppermute | solution.py:344
  207.6 112.0 %reduce-scatter.11.cloned.1.call-start = ((), (), s32[]{:S(2)}) async-start(), calls=%async_computation.9 | async-start | bytes 1990656 | tf_op jit(solution)/shard_map/reduce_scatter | solution.py:362
  226.7 137.2 %reduce-scatter.9.cloned.1.call-start = ((), (), s32[]{:S(2)}) async-start(), calls=%async_computation.8 | async-start | bytes 3981312 | tf_op jit(solution)/shard_map/reduce_scatter | solution.py:362
  254.7 143.8 %reduce-scatter.7.cloned.1.call-start = ((), (), s32[]{:S(2)}) async-start(), calls=%async_computation.6 | async-start | bytes 1990656 | tf_op jit(solution)/shard_map/reduce_scatter | solution.py:362
  259.8 2.6 collective-permute-start.30
  261.9 3.1 collective-permute-start.33
  262.4 28.3 %collective-permute-start.29 = (bf16[288,1152]{1,0:T(8,128)(2,1)}, bf16[288,1152]{1,0:T(8,128)(2,1)}, u32[]{:S(2)}, u32[]{:S(2)}) collective-permute-start(bf16[288,1152]{1,0:T(8,128)(2,1)} %get-tuple-element.77), channel_id=1, source_target_pairs={{0,1},{1,0},{2,3},{3,2},{4,5},{5,4},{6,7},{7,6},{8,9},{9,8},{10,11... | collective-permute-start | bytes 1990664 | tf_op jit(solution)/shard_map/ppermute | solution.py:344
  263.4 27.3 %collective-permute-start.31 = (bf16[288,1152]{1,0:T(8,128)(2,1)}, bf16[288,1152]{1,0:T(8,128)(2,1)}, u32[]{:S(2)}, u32[]{:S(2)}) collective-permute-start(bf16[288,1152]{1,0:T(8,128)(2,1)} %add_convert_fusion.4), channel_id=1, source_target_pairs={{0,2},{1,3},{2,0},{3,1},{4,6},{5,7},{6,4},{7,5},{8,10},{9,11},{10,... | collective-permute-start | bytes 1990664 | tf_op jit(solution)/shard_map/ppermute | solution.py:344
  263.7 30.8 %collective-permute-start.32 = (bf16[288,1152]{1,0:T(8,128)(2,1)}, bf16[288,1152]{1,0:T(8,128)(2,1)}, u32[]{:S(2)}, u32[]{:S(2)}) collective-permute-start(bf16[288,1152]{1,0:T(8,128)(2,1)} %get-tuple-element.83), channel_id=1, source_target_pairs={{0,1},{1,0},{2,3},{3,2},{4,5},{5,4},{6,7},{7,6},{8,9},{9,8},{10,11... | collective-permute-start | bytes 1990664 | tf_op jit(solution)/shard_map/ppermute | solution.py:344
  266.1 29.2 %collective-permute-start.34 = (bf16[288,1152]{1,0:T(8,128)(2,1)}, bf16[288,1152]{1,0:T(8,128)(2,1)}, u32[]{:S(2)}, u32[]{:S(2)}) collective-permute-start(bf16[288,1152]{1,0:T(8,128)(2,1)} %add_convert_fusion.2), channel_id=1, source_target_pairs={{0,2},{1,3},{2,0},{3,1},{4,6},{5,7},{6,4},{7,5},{8,10},{9,11},{10,... | collective-permute-start | bytes 1990664 | tf_op jit(solution)/shard_map/ppermute | solution.py:344
  290.6 2.3 collective-permute-start.36
  292.4 4.5 collective-permute-start.35
  293.0 12.2 %collective-permute-start.37 = (bf16[288,768]{1,0:T(8,128)(2,1)S(1)}, bf16[288,768]{1,0:T(8,128)(2,1)S(1)}, u32[]{:S(2)}, u32[]{:S(2)}) collective-permute-start(bf16[288,768]{1,0:T(8,128)(2,1)S(1)} %add_convert_fusion.9), channel_id=1, source_target_pairs={{0,2},{1,3},{2,0},{3,1},{4,6},{5,7},{6,4},{7,5},{8,10},{9,11},{10,... | collective-permute-start | bytes 1327112 | tf_op jit(solution)/shard_map/ppermute | solution.py:344
  307.0 124.8 %all-gather.10.cloned.1.call-start = ((), (), s32[]{:S(2)}) async-start(), calls=%async_computation.10 | async-start | bytes 1990656 | tf_op jit(solution)/shard_map/all_gather | solution.py:367
  319.6 154.6 %all-gather.12.cloned.1.call-start = ((), (), s32[]{:S(2)}) async-start(), calls=%async_computation.11 | async-start | bytes 3981312 | tf_op jit(solution)/shard_map/all_gather | solution.py:367
  363.9 5.0 collective-permute-start.38
  368.9 139.4 %all-gather.8.cloned.1.call-start = ((), (), s32[]{:S(2)}) async-start(), calls=%async_computation.7 | async-start | bytes 1990656 | tf_op jit(solution)/shard_map/all_gather | solution.py:367
  373.8 10.7 %collective-permute-start.22 = (bf16[256,1152]{1,0:T(8,128)(2,1)S(1)}, bf16[256,1152]{1,0:T(8,128)(2,1)S(1)}, u32[]{:S(2)}, u32[]{:S(2)}) collective-permute-start(bf16[256,1152]{1,0:T(8,128)(2,1)S(1)} %get-tuple-element.142), channel_id=1, source_target_pairs={{0,1},{1,0},{2,3},{3,2},{4,5},{5,4},{6,7},{7,6},{8,9},{9,8},{10,11... | collective-permute-start | bytes 1769480 | tf_op jit(solution)/shard_map/ppermute | solution.py:344
  378.0 33.5 %collective-permute-start.21 = (bf16[256,1152]{1,0:T(8,128)(2,1)}, bf16[256,1152]{1,0:T(8,128)(2,1)}, u32[]{:S(2)}, u32[]{:S(2)}) collective-permute-start(bf16[256,1152]{1,0:T(8,128)(2,1)} %get-tuple-element.141), channel_id=1, source_target_pairs={{0,1},{1,0},{2,3},{3,2},{4,5},{5,4},{6,7},{7,6},{8,9},{9,8},{10,11... | collective-permute-start | bytes 1769480 | tf_op jit(solution)/shard_map/ppermute | solution.py:344
  382.8 28.8 %copy-start.16 = (f32[256,1152]{1,0:T(8,128)S(1)}, f32[256,1152]{1,0:T(8,128)}, u32[]{:S(2)}) copy-start(f32[256,1152]{1,0:T(8,128)} %copy-done.15) | copy-start | bytes 3538948
  382.8 15.7 %collective-permute-start.24 = (f32[2,1152]{1,0:T(2,128)S(1)}, f32[2,1152]{1,0:T(2,128)S(1)}, u32[]{:S(2)}, u32[]{:S(2)}) collective-permute-start(f32[2,1152]{1,0:T(2,128)S(1)} %pad_maximum_fusion.5), channel_id=1, source_target_pairs={{0,1},{1,0},{2,3},{3,2},{4,5},{5,4},{6,7},{7,6},{8,9},{9,8},{10,11... | collective-permute-start | bytes 27656 | tf_op jit(solution)/shard_map/ppermute | solution.py:344
  385.5 26.1 %collective-permute-start.23 = (bf16[256,1152]{1,0:T(8,128)(2,1)}, bf16[256,1152]{1,0:T(8,128)(2,1)}, u32[]{:S(2)}, u32[]{:S(2)}) collective-permute-start(bf16[256,1152]{1,0:T(8,128)(2,1)} %add_convert_fusion.6), channel_id=1, source_target_pairs={{0,2},{1,3},{2,0},{3,1},{4,6},{5,7},{6,4},{7,5},{8,10},{9,11},{10,... | collective-permute-start | bytes 1769480 | tf_op jit(solution)/shard_map/ppermute | solution.py:344
  398.5 3.7 collective-permute-start.25
  402.3 7.8 %collective-permute-start.26 = (f32[2,1152]{1,0:T(2,128)S(1)}, f32[2,1152]{1,0:T(2,128)S(1)}, u32[]{:S(2)}, u32[]{:S(2)}) collective-permute-start(f32[2,1152]{1,0:T(2,128)S(1)} %fusion.39), channel_id=1, source_target_pairs={{0,4},{4,0},{8,12},{12,8},{16,20},{20,16},{24,28},{28,24},{1,5},{5... | collective-permute-start | bytes 27656 | tf_op jit(solution)/shard_map/ppermute | solution.py:661
  410.1 4.0 collective-permute-start.27
  414.0 24.1 %collective-permute-start.28 = (f32[2,1152]{1,0:T(2,128)S(1)}, f32[2,1152]{1,0:T(2,128)S(1)}, u32[]{:S(2)}, u32[]{:S(2)}) collective-permute-start(f32[2,1152]{1,0:T(2,128)S(1)} %add.180), channel_id=1, source_target_pairs={{0,16},{4,20},{8,24},{12,28},{16,0},{20,4},{24,8},{28,12},{1,17},{... | collective-permute-start | bytes 27656 | tf_op jit(solution)/shard_map/ppermute | solution.py:661
  (47 other events, 146.7 us)
Sparse Core Ops, SparseCore 0:
  32.1 39.9 all-gather.5
  207.8 77.8 reduce-scatter.4
  288.0 31.5 reduce-scatter.10
  322.4 41.4 reduce-scatter.8
  366.7 31.7 reduce-scatter.6
  399.9 31.8 all-gather.9
  433.4 40.8 all-gather.11
  475.9 32.4 all-gather.7
